TPU v7x, 128 devices: a whole 4x4x4 slice. The times are simulated.
128 devices in a mesh: seq: 16 (over x, y_hi, core), tp: 8 (over z, y_lo).
Axes of the slice: x: 4, y: 4 (y_hi: 2, y_lo: 2; y = y_hi * 2 + y_lo), z: 4, core: 2. Of those that a mesh axis runs over, the one named last changes fastest.
Arguments:
- byte_ids: int32 [4096, 8], P('seq'), may hold values from 0 to 255
- global_out: bfloat16 [4096, 8192], P('seq', 'tp'), may hold values from -6 to 6
- global_in_grad: bfloat16 [4096, 8192], P('seq', 'tp'), may hold values from -6 to 6
- out_grad: bfloat16 [32768, 1024], P(('seq', 'tp')), may hold values from -6 to 6
- proj_weight: bfloat16 [1024, 1024], replicated, may hold values from -0.1875 to 0.1875
- emb_local: bfloat16 [256, 1024], replicated, may hold values from -6 to 6
- norm_gain: float32 [1024], replicated, may hold values from 0.1 to 1.9
- up_weight: bfloat16 [1024, 2048], replicated, may hold values from -0.1875 to 0.1875
- down_weight: bfloat16 [2048, 1024], replicated, may hold values from -0.125 to 0.125
Outputs:
- glob_out_grad: bfloat16 [4096, 8192], P('seq', 'tp')
- emb_global_grad: float32 [256, 1024], replicated
- emb_local_grad: float32 [256, 1024], replicated
- gain_grad: float32 [1024], replicated
- proj_grad: float32 [1024, 1024], P(None, ('seq', 'tp'))
- up_grad: float32 [1024, 2048], P(None, ('seq', 'tp'))
- down_grad: float32 [2048, 1024], P(('seq', 'tp'))
All inputs are finite; a program needn't handle non-finite values.
Results may differ from a plain program's by a relative error of at most 0.015.
Values may be sent and summed in bfloat16 or wider, within the bound.
A program may use at most 128 MiB of HBM per device.

v0:
```python
import jax
import jax.numpy as jnp
from jax import lax
from jax.sharding import PartitionSpec as P


def inner(left, right):
    return lax.dot_general(
        left, right, (((0,), (0,)), ((), ())), preferred_element_type=jnp.float32
    )


def outer(left, right):
    return lax.dot_general(
        left, right, (((1,), (1,)), ((), ())), preferred_element_type=jnp.float32
    )


def on_device(
    byte_ids,
    global_out,
    global_in_grad,
    out_grad,
    proj_weight,
    emb_local,
    norm_gain,
    up_weight,
    down_weight,
):
    tp_count = lax.axis_size("tp")
    tp_place = lax.axis_index("tp")
    patch = byte_ids.shape[1]
    slot = proj_weight.shape[0]
    vocab = emb_local.shape[0]
    local_patches = global_out.shape[0] // tp_count
    local_ids = lax.dynamic_slice_in_dim(byte_ids, tp_place * local_patches, local_patches, 0)
    local_out = lax.all_to_all(global_out, "tp", split_axis=0, concat_axis=1, tiled=True)
    slot_in = local_out.reshape(local_patches * patch, slot)
    first = jnp.full((local_patches, 1), -1, jnp.int32)
    prev_id = jnp.concatenate([first, local_ids[:, :-1]], axis=1).reshape(-1)
    prev_hot = jax.nn.one_hot(prev_id, vocab, dtype=jnp.bfloat16)
    u_rows = jnp.dot(slot_in, proj_weight, preferred_element_type=jnp.float32) + jnp.dot(
        prev_hot, emb_local, preferred_element_type=jnp.float32
    )
    scale = lax.rsqrt(jnp.mean(u_rows * u_rows, axis=1, keepdims=True) + 1e-05)
    normed = u_rows * scale
    r_rows = (normed * norm_gain).astype(jnp.bfloat16)
    a_rows = jnp.dot(r_rows, up_weight, preferred_element_type=jnp.float32)
    sig = jax.nn.sigmoid(a_rows)
    h_rows = (a_rows * sig).astype(jnp.bfloat16)
    dh_rows = outer(out_grad, down_weight)
    da_rows = (dh_rows * sig * (1.0 + a_rows * (1.0 - sig))).astype(jnp.bfloat16)
    dr_rows = outer(da_rows, up_weight)
    dn_rows = dr_rows * norm_gain
    du_rows = (
        out_grad.astype(jnp.float32)
        + scale * (dn_rows - normed * jnp.mean(dn_rows * normed, axis=1, keepdims=True))
    ).astype(jnp.bfloat16)
    local_back = (
        outer(du_rows, proj_weight).astype(jnp.bfloat16).reshape(local_patches, patch * slot)
    )
    glob_out_grad = lax.all_to_all(local_back, "tp", split_axis=1, concat_axis=0, tiled=True)
    slots_here = patch // tp_count
    own_ids = lax.dynamic_slice_in_dim(byte_ids, tp_place * slots_here, slots_here, 1).reshape(-1)
    own_hot = jax.nn.one_hot(own_ids, vocab, dtype=jnp.bfloat16)
    emb_global_part = inner(own_hot, global_in_grad)
    emb_local_part = inner(prev_hot, du_rows)
    gain_part = jnp.sum(dr_rows * normed, axis=0)
    emb_global_grad, emb_local_grad, gain_grad = lax.psum(
        (emb_global_part, emb_local_part, gain_part), ("seq", "tp")
    )
    proj_part = inner(slot_in, du_rows)
    up_part = inner(r_rows, da_rows)
    down_part = inner(h_rows, out_grad)
    proj_grad, up_grad, down_grad = (
        lax.psum_scatter(proj_part, ("seq", "tp"), scatter_dimension=1, tiled=True),
        lax.psum_scatter(up_part, ("seq", "tp"), scatter_dimension=1, tiled=True),
        lax.psum_scatter(down_part, ("seq", "tp"), scatter_dimension=0, tiled=True),
    )
    return (
        glob_out_grad,
        emb_global_grad,
        emb_local_grad,
        gain_grad,
        proj_grad,
        up_grad,
        down_grad,
    )


def solution(mesh):
    placed = (
        P("seq", None),
        P("seq", "tp"),
        P("seq", "tp"),
        P(("seq", "tp"), None),
        P(),
        P(),
        P(),
        P(),
        P(),
    )
    return jax.shard_map(
        on_device,
        mesh=mesh,
        in_specs=placed,
        out_specs=(
            P("seq", "tp"),
            P(),
            P(),
            P(),
            P(None, ("seq", "tp")),
            P(None, ("seq", "tp")),
            P(("seq", "tp"), None),
        ),
        check_vma=False,
    )
```

profile of v0, /device:TPU:1, one launch (start us, length us, event | category | flops | bytes accessed | tf_op | source)
XLA Modules:
  0.0 2147.1 jit_solution(6053280185825184937)
XLA Ops:
  7.2 7.0 all-to-all-start
  14.2 0.8 constant_dynamic-slice_fusion.1
  15.3 0.7 constant_dynamic-slice_fusion
  16.0 2.4 fusion.11
  18.4 5.0 all-to-all-done
  23.4 0.8 copy-done.1
  24.2 0.8 fusion.6
  25.1 0.4 multiply_reduce_fusion.2
  25.5 0.9 copy-done.4
  26.5 1.3 fusion.17
  27.8 1.0 copy-done.12
  28.8 1.5 fusion.1
  30.4 1.5 multiply_reduce_fusion
  31.9 0.3 add_convert_fusion
  32.2 0.8 copy-done.2
  33.0 1.4 fusion.10
  34.5 4.0 convolution_bitcast_fusion
  38.5 5.8 fusion.16
  44.4 1.0 copy-done.10
  45.4 6.2 fusion.3
  51.6 1.0 copy-done.3
  52.6 0.7 fusion.2
  53.4 1.1 copy.24
  54.5 3.5 all-to-all-start.1
  58.0 67.8 %psum.23 = f32[1024]{0:T(1024)} all-reduce(f32[1024]{0:T(1024)S(1)} %get-tuple-element.7), channel_id=1, replica_groups=mesh['seq'=16,'tp'=8] {'seq','tp'}, use_global_device_ids=true, to_apply=%region_5.6 | all-reduce | flops 1024 | bytes 8192 | tf_op jit(solution)/shard_map/psum | solution.py:69
  125.8 62.3 %all-reduce.4.cloned.1.call-done = (f32[256,1024]{1,0:T(8,128)}, f32[256,1024]{1,0:T(8,128)}) async-done(((f32[256,1024]{1,0:T(8,128)}, f32[256,1024]{1,0:T(8,128)}), (f32[256,1024]{1,0:T(8,128)}, f32[256,1024]{1,0:T(8,128)})) %all-reduce.4.cloned.1.call-update) | async-done | bytes 2097168 | tf_op jit(solution)/shard_map/psum | solution.py:69
  188.0 636.1 %reduce-scatter.4.cloned.1.call-done = f32[1024,8]{0,1:T(8,128)} async-done(((f32[1024,1024]{0,1:T(8,128)}), f32[1024,8]{0,1:T(8,128)}) %reduce-scatter.4.cloned.1.call-update) | async-done | bytes 32784 | tf_op jit(solution)/shard_map/reduce_scatter | solution.py:76
  824.1 656.3 %reduce-scatter.6.cloned.1.call-done = f32[1024,16]{0,1:T(8,128)} async-done(((f32[1024,2048]{0,1:T(8,128)}), f32[1024,16]{0,1:T(8,128)}) %reduce-scatter.6.cloned.1.call-update) | async-done | bytes 65552 | tf_op jit(solution)/shard_map/reduce_scatter | solution.py:77
  1480.5 656.1 %reduce-scatter.8.cloned.1.call-done = f32[16,1024]{1,0:T(8,128)} async-done(((f32[2048,1024]{1,0:T(8,128)}), f32[16,1024]{1,0:T(8,128)}) %reduce-scatter.8.cloned.1.call-update) | async-done | bytes 65552 | tf_op jit(solution)/shard_map/reduce_scatter | solution.py:78
  2136.5 0.8 copy.37
  2137.3 2.3 copy.38
  2139.6 1.0 copy.39
  (34 shorter events, 0.5 us)
Async XLA Ops:
  7.2 17.1 copy-start
  7.2 16.2 all-to-all-start
  14.2 173.8 %all-reduce.4.cloned.1.call-start = ((), (), s32[]{:S(2)}) async-start(), calls=%async_computation.8 | async-start | bytes 4194304 | tf_op jit(solution)/shard_map/psum | solution.py:69
  23.4 0.8 copy-start.1
  23.4 1.6 copy-start.8
  24.2 2.2 copy-start.4
  25.1 1.4 copy-start.11
  26.4 1.3 copy-start.9
  26.4 2.4 copy-start.12
  28.8 1.6 copy-start.5
  30.4 1.5 copy-start.6
  32.2 0.8 copy-start.2
  34.4 789.7 %reduce-scatter.4.cloned.1.call-start = ((), (), s32[]{:S(2)}) async-start(), calls=%async_computation.5 | async-start | bytes 4227072 | tf_op jit(solution)/shard_map/reduce_scatter | solution.py:76
  38.5 1442.0 %reduce-scatter.6.cloned.1.call-start = ((), (), s32[]{:S(2)}) async-start(), calls=%async_computation.6 | async-start | bytes 8454144 | tf_op jit(solution)/shard_map/reduce_scatter | solution.py:77
  44.3 1.0 copy-start.10
  44.4 2092.2 %reduce-scatter.8.cloned.1.call-start = ((), (), s32[]{:S(2)}) async-start(), calls=%async_computation.7 | async-start | bytes 8454144 | tf_op jit(solution)/shard_map/reduce_scatter | solution.py:78
  51.6 1.1 copy-start.3
  54.5 71.3 %all-to-all-start.1 = ((bf16[32,8,1024]{2,0,1:T(8,128)(2,1)}), bf16[32,8,1024]{2,0,1:T(8,128)(2,1)S(1)}, u32[]{:S(2)}, u32[]{:S(2)}) async-start(bf16[32,8,1024]{2,0,1:T(8,128)(2,1)} %copy.24), calls=%async_computation.1 | async-start | bytes 1048576 | tf_op jit(solution)/shard_map/all_to_all | solution.py:62
  2136.5 3.1 copy-start.7
Sparse Core Ops, SparseCore 0:
  34.5 153.4 all-reduce.3
  191.0 633.1 reduce-scatter.3
  827.1 653.3 reduce-scatter.5
  1483.3 653.2 reduce-scatter.7
where the time goes:
time: 2160 us; the launch traced here: 2150 us
  waiting for transfers between devices  2020 us (94%)
  blocking collectives  67.8 us (3%)
  matrix products  26.1 us (1%)
    reduce_scatter x1, waiting for transfers between devices, on_device(): lax.psum_scatter(up_part, ('seq', 'tp'), scatter_dimension=1, tiled=True)  656 us
    reduce_scatter x1, waiting for transfers between devices, on_device(): lax.psum_scatter(down_part, ('seq', 'tp'), scatter_dimension=0, tiled=True)  656 us
    reduce_scatter x1, waiting for transfers between devices, on_device(): lax.psum_scatter(proj_part, ('seq', 'tp'), scatter_dimension=1, tiled=True)  636 us
    psum x1, blocking collectives, on_device(): lax.psum((emb_global_part, emb_local_part, gain_part), ('seq', 'tp'))  67.8 us
    psum x1, waiting for transfers between devices, on_device(): lax.psum((emb_global_part, emb_local_part, gain_part), ('seq', 'tp'))  62.3 us
  transfers between devices with their start and end apart: 6, of which 5 were waited for; matrix products, arithmetic and copies ran while one was open for 1% of the time, Pallas kernels for 0%

commit v1 on v0

v1 whole, which is shorter than its diff:
```python
import functools

import jax
import jax.numpy as jnp
from jax import lax
from jax.experimental import pallas as pl
from jax.experimental.pallas import tpu as pltpu
from jax.sharding import PartitionSpec as P

BF = jnp.bfloat16
F32 = jnp.float32
MESH = pl.DeviceIdType.MESH
ALL = slice(None)
D_UNITS = ((0, 384, (0, 1, 2)), (384, 384, (1, 2, 0)), (768, 256, (2, 0, 1)))
M_UNITS = ((512, 256, (0, 1, 2)), (0, 256, (1, 2, 0)), (256, 256, (2, 0, 1)))
U_UNITS = ((0, 256, (0, 1, 2)), (256, 384, (1, 2, 0)), (640, 384, (2, 0, 1)))
ALL_UNITS = D_UNITS + M_UNITS + U_UNITS
M_WIDTH = 768


def mm(a, b):
    return lax.dot_general(a, b, (((1,), (0,)), ((), ())), preferred_element_type=F32)


def mm_nt(a, b):
    return lax.dot_general(a, b, (((1,), (1,)), ((), ())), preferred_element_type=F32)


def mm_tn(a, b):
    return lax.dot_general(a, b, (((0,), (0,)), ((), ())), preferred_element_type=F32)


def iota(shape, dim):
    return lax.broadcasted_iota(jnp.int32, shape, dim)


def remote(src, dst, send, recv, device):
    return pltpu.make_async_remote_copy(
        src_ref=src, dst_ref=dst, send_sem=send, recv_sem=recv, device_id=device, device_id_type=MESH
    )


class Ring:
    def __init__(self, src, axes, cols, over, half, spot, device_at, bufs, out, send, recv, base):
        self.src, self.axes, self.cols, self.over, self.half = src, axes, cols, over, half
        self.bufs, self.out, self.spot = bufs, out, spot
        here = spot[over]
        self.here, self.right, self.left, self.far = here, (here + 1) % 4, (here + 3) % 4, (here + 2) % 4
        self.to_right = device_at(over, self.right)
        self.to_left = device_at(over, self.left)
        self.sems = [(send.at[base + i], recv.at[base + i]) for i in range(6)]

    def part(self, place, half):
        index = tuple(
            place if a == self.over else pl.ds(2 * half, 2) if a == self.half else ALL for a in self.axes
        )
        cols = ALL if self.cols is None else pl.ds(*self.cols)
        return self.src.at[index + (ALL, cols)]

    def start(self):
        rel_a, rel_b, dir_a, dir_b, fin_a, fin_b = self.bufs
        s = self.sems
        self.c1 = remote(self.part(self.far, 0), rel_a, *s[0], self.to_right)
        self.d1 = remote(self.part(self.far, 1), rel_b, *s[1], self.to_left)
        self.c2 = remote(self.part(self.right, 1), dir_b, *s[2], self.to_right)
        self.d2 = remote(self.part(self.left, 0), dir_a, *s[3], self.to_left)
        self.c3 = remote(rel_a, fin_a, *s[4], self.to_right)
        self.d3 = remote(rel_b, fin_b, *s[5], self.to_left)
        for copy in (self.c1, self.d1, self.c2, self.d2):
            copy.start()

    def relay(self):
        rel_a, rel_b = self.bufs[:2]
        self.c1.wait_recv()
        rel_a[...] = (rel_a[...].astype(F32) + self.part(self.right, 0)[...].astype(F32)).astype(BF)
        self.c3.start()
        self.d1.wait_recv()
        rel_b[...] = (rel_b[...].astype(F32) + self.part(self.left, 1)[...].astype(F32)).astype(BF)
        self.d3.start()

    def out_half(self, half):
        index = tuple(pl.ds(2 * half, 2) if a == self.half else ALL for a in self.axes if a != self.over)
        return self.out.at[index]

    def finish(self):
        _, _, dir_a, dir_b, fin_a, fin_b = self.bufs
        self.d2.wait_recv()
        self.c3.wait_recv()
        self.out_half(0)[...] = (
            self.part(self.here, 0)[...].astype(F32) + fin_a[...].astype(F32) + dir_a[...].astype(F32)
        ).astype(BF)
        self.c2.wait_recv()
        self.d3.wait_recv()
        self.out_half(1)[...] = (
            self.part(self.here, 1)[...].astype(F32) + fin_b[...].astype(F32) + dir_b[...].astype(F32)
        ).astype(BF)

    def drain(self):
        for copy in (self.c1, self.d1, self.c2, self.d2, self.c3, self.d3):
            copy.wait_send()


class Unit:
    def __init__(self, src, cols, order, spot, device_at, bufs, send, recv):
        a, b, c = order
        first, second, out1, out2, last = bufs
        rest = tuple(n for n in (0, 1, 2) if n != a)
        self.one = Ring(src, (0, 1, 2), cols, a, b, spot, device_at, first, out1, send, recv, 0)
        self.two = Ring(out1, rest, None, b, c, spot, device_at, second, out2, send, recv, 6)
        self.out2, self.last = out2, last
        self.here = spot[c]
        self.copies = []
        for k in (2, 1, 3):
            there = (self.here + k) % 4
            self.copies.append(
                remote(
                    out2.at[there],
                    last.at[k - 1],
                    send.at[11 + k],
                    recv.at[11 + k],
                    device_at(c, there),
                )
            )

    def start3(self):
        for copy in self.copies:
            copy.start()

    def finish3(self):
        for copy in self.copies:
            copy.wait_recv()
        total = self.out2[self.here].astype(F32)
        for k in range(3):
            total = total + self.last[k].astype(F32)
        return total

    def drain(self):
        self.one.drain()
        self.two.drain()
        for copy in self.copies:
            copy.wait_send()


def unit_scratch(width, order):
    a, b, c = order
    rest = tuple(n for n in (0, 1, 2) if n != a)
    one = tuple(2 if n == b else 4 for n in rest)
    return (
        [pltpu.VMEM(one + (16, width), BF)] * 6
        + [pltpu.VMEM((2, 16, width), BF)] * 6
        + [pltpu.VMEM((4, 4, 16, width), BF), pltpu.VMEM((4, 16, width), BF), pltpu.VMEM((3, 16, width), BF)]
    )


FIXED = (
    ("og", (256, 1024), BF),
    ("dn", (2048, 1024), BF),
    ("gig", (256, 1024), BF),
    ("pw", (1024, 1024), BF),
    ("emb", (256, 1024), BF),
    ("up", (1024, 2048), BF),
    ("og2", (2, 256, 1024), BF),
    ("slot", (8, 32, 1024), BF),
    ("dh", (8, 256, 256), F32),
    ("norm", (256, 1024), F32),
    ("scale", (256, 128), F32),
    ("r2", (2, 256, 1024), BF),
    ("hot", (256, 256), BF),
    ("ht", (2, 1024, 256), BF),
    ("hr", (1024, 256), BF),
    ("dat", (2, 1024, 256), BF),
    ("dar", (1024, 256), BF),
    ("da", (256, 2048), BF),
    ("dr", (256, 1024), F32),
    ("du", (256, 1024), BF),
    ("dut", (1024, 256), BF),
    ("dp", (4, 4, 4, 16, 1024), BF),
    ("upart", (4, 4, 4, 16, 1024), BF),
    ("mp", (2, 4, 4, 4, 16, M_WIDTH), BF),
    ("mr", (4, 4, 4, 16, M_WIDTH), BF),
    ("gog", (8, 32, 1024), BF),
    ("agb", (2, 4, 4, 4, 16, 256), BF),
    ("gp", (4, 4, 8, 1024), F32),
)


def kernel(*refs):
    ids, go_h, gig_h, og_h, pw_h, emb_h, gain, up_h, dn_h = refs[:9]
    gog_o, embg_o, embl_o, gain_o, proj_o, up_o, down_o = refs[9:16]
    rest = list(refs[16:])
    buf = {name: rest.pop(0) for name, _, _ in FIXED}
    unit_bufs = []
    for _ in ALL_UNITS:
        mine = [rest.pop(0) for _ in range(15)]
        unit_bufs.append((mine[:6], mine[6:12], mine[12], mine[13], mine[14]))
    load_sem, x_send, x_recv, a_send, a_recv, b_send, b_recv, u_send, u_recv, g_send, g_recv, q_send, q_recv = rest
    og, dn, gig, pw, emb, up = (buf[n] for n in ("og", "dn", "gig", "pw", "emb", "up"))
    og2, slot, dh, norm, scale, r2 = (buf[n] for n in ("og2", "slot", "dh", "norm", "scale", "r2"))
    hot, ht, hr, dat, dar, da = (buf[n] for n in ("hot", "ht", "hr", "dat", "dar", "da"))
    dr, du, dut, dp, upart, mp = (buf[n] for n in ("dr", "du", "dut", "dp", "upart", "mp"))
    mr, gog, agb, gp = (buf[n] for n in ("mr", "gog", "agb", "gp"))

    seq = lax.axis_index("seq")
    tp = lax.axis_index("tp")
    core = seq % 2
    other = 1 - core
    x = seq // 4
    y = (seq // 2) % 2 * 2 + tp % 2
    z = tp // 2
    spot = (x, y, z)

    def device(px, py, pz, pc):
        return ((px * 2 + py // 2) * 2 + pc, pz * 2 + py % 2)

    def device_at(axis, place):
        where = list(spot)
        where[axis] = place
        return device(*where, core)

    partner = device(x, y, z, other)

    barrier = pltpu.get_barrier_semaphore()
    pl.semaphore_signal(barrier, inc=1, device_id=partner, device_id_type=MESH)
    for k in range(1, 8):
        pl.semaphore_signal(barrier, inc=1, device_id=(seq, (tp + k) % 8), device_id_type=MESH)
    for axis in range(3):
        for k in range(1, 4):
            pl.semaphore_signal(
                barrier, inc=1, device_id=device_at(axis, (spot[axis] + k) % 4), device_id_type=MESH
            )
    loads = {}
    for n, (name, src, dst) in enumerate(
        (
            ("og", og_h, og),
            ("dn", dn_h, dn),
            ("gig", gig_h, gig),
            ("pw", pw_h, pw),
            ("emb", emb_h, emb),
            ("up", up_h, up),
            ("own", go_h.at[tp], slot.at[tp]),
        )
    ):
        loads[name] = pltpu.make_async_copy(src, dst, load_sem.at[n])
        loads[name].start()
    pl.semaphore_wait(barrier, 17)

    fetch = [
        remote(go_h.at[(tp + k) % 8], slot.at[tp], a_send.at[k - 1], a_recv.at[k - 1], (seq, (tp + k) % 8))
        for k in range(1, 8)
    ]
    for copy in fetch:
        copy.start()

    def swap(n, src, dst):
        copy = remote(src, dst, x_send.at[n], x_recv.at[n], partner)
        copy.start()
        return copy

    loads["og"].wait()
    row, col = iota((256, 256), 0), iota((256, 256), 1)
    perm = (col == 8 * (row % 32) + row // 32).astype(BF)
    og2[0] = mm(perm, og[...]).astype(BF)
    x_og = swap(0, og2.at[0], og2.at[1])

    loads["dn"].wait()

    def dh_step(n, carry):
        at = pl.ds(pl.multiple_of(n * 256, 256), 256)
        dh[n] = mm_nt(og2[0], dn[at, :])
        return carry

    lax.fori_loop(0, 8, dh_step, 0)

    ids_v = ids[...]
    own_id = jnp.sum(jnp.where(iota((8, 256), 0) == tp, ids_v, 0), axis=0, keepdims=True)
    hot_own = (row == own_id).astype(BF)
    pick = (row == tp * 32 + col % 32).astype(BF)
    ids_here = mm(ids_v.astype(F32).astype(BF), pick)
    col8 = iota((8, 256), 1)
    prev = jnp.sum(jnp.where(iota((8, 256), 0) == col8 // 32 - 1, ids_here, 0.0), axis=0, keepdims=True)
    prev_id = jnp.where(iota((1, 256), 1) < 32, -1, prev.astype(jnp.int32))
    hot[...] = (row == prev_id).astype(BF)

    def put_table(n, value, first):
        block = value.astype(BF).reshape(4, 2, 2, 16, 256)
        for c in range(2):
            for yh in range(2):
                for yl in range(2):
                    mp[c, :, yh * 2 + yl, n, :, pl.ds(first, 128)] = block[:, yh, c, :, yl * 128 : yl * 128 + 128]

    loads["gig"].wait()
    for n in range(4):
        put_table(n, mm(hot_own, gig[:, n * 256 : n * 256 + 256]), 640)
    x_eg = swap(1, mp.at[other, :, :, :, :, pl.ds(640, 128)], mr.at[:, :, :, :, pl.ds(640, 128)])

    loads["pw"].wait()
    loads["emb"].wait()
    loads["own"].wait()
    for copy in fetch:
        copy.wait_recv()

    square = jnp.zeros((256, 1), F32)
    slot_v = slot[...].reshape(256, 1024)
    for n in range(4):
        at = slice(n * 256, n * 256 + 256)
        u_part = mm(slot_v, pw[:, at]) + mm_tn(hot[...], emb[:, at])
        norm[:, at] = u_part
        square = square + jnp.sum(u_part * u_part, axis=1, keepdims=True)
    scale_v = lax.rsqrt(square * (1.0 / 1024.0) + 1e-05)
    scale[...] = jnp.broadcast_to(scale_v, (256, 128))
    for n in range(4):
        at = slice(n * 256, n * 256 + 256)
        normed = norm[:, at] * scale_v
        norm[:, at] = normed
        r2[0, :, at] = (normed * gain[:, at]).astype(BF)
    x_r = swap(2, r2.at[0], r2.at[1])

    loads["up"].wait()

    def ff_step(k, carry):
        at = pl.ds(pl.multiple_of(k * 256, 256), 256)
        rows = pl.ds(pl.multiple_of(k * 128, 128), 128)
        a = mm(r2[0], up[:, at])
        sig = jax.nn.sigmoid(a)
        h_t = (a * sig).astype(BF).T
        ht[0, rows, :] = h_t[:128]
        ht[1, rows, :] = h_t[128:]
        da_v = (dh[k] * sig * (1.0 + a * (1.0 - sig))).astype(BF)
        da[:, at] = da_v
        da_t = da_v.T
        dat[0, rows, :] = da_t[:128]
        dat[1, rows, :] = da_t[128:]
        return carry

    lax.fori_loop(0, 8, ff_step, 0)
    x_h = swap(3, ht.at[other], hr)
    x_da = swap(4, dat.at[other], dar)

    def units(src, table, first):
        return [
            Unit(src, cols_of(t), t[2], spot, device_at, unit_bufs[first + i], u_send.at[first + i], u_recv.at[first + i])
            for i, t in enumerate(table)
        ]

    def cols_of(entry):
        return entry[0], entry[1]

    d_units = units(dp, D_UNITS, 0)
    m_units = units(mr, M_UNITS, 3)
    u_units = units(upart, U_UNITS, 6)

    def big(lhs, lhs_far, rhs, out, table):
        done = 0
        for n in range(4):
            at = slice(n * 256, n * 256 + 256)

            def step(g, carry):
                rows = pl.ds(pl.multiple_of(g * 512, 512), 512)
                v = mm(lhs[core, rows, :], rhs[0, :, at]) + mm(lhs_far[rows, :], rhs[1, :, at])
                v = v.astype(BF).reshape(2, 2, 4, 2, 16, 256)
                for xx in range(2):
                    for yh in range(2):
                        for yl in range(2):
                            out[2 * g + xx, yh * 2 + yl, :, :, at] = v[xx, yh, :, yl]
                return carry

            lax.fori_loop(0, 2, step, 0)
            while done < 3 and table[done].one.cols[0] + table[done].one.cols[1] <= n * 256 + 256:
                table[done].one.start()
                done += 1

    x_og.wait_recv()
    x_h.wait_recv()
    big(ht, hr, og2, dp, d_units)

    for n in range(4):
        at = slice(n * 256, n * 256 + 256)
        dr[:, at] = mm_nt(da[...], up[at, :])
    for unit in d_units:
        unit.one.relay()

    gain_v = gain[...]

    def du_step(i, total):
        rows = pl.ds(pl.multiple_of(i * 32, 32), 32)
        dr_v = dr[rows, :]
        normed = norm[rows, :]
        product = dr_v * normed
        dn_v = dr_v * gain_v
        mean = jnp.sum(product * gain_v, axis=1, keepdims=True) * (1.0 / 1024.0)
        du_v = og2[0, rows, :].astype(F32) + scale[rows, 0:1] * (dn_v - normed * mean)
        du[rows, :] = du_v.astype(BF)
        return total + jnp.sum(product.reshape(4, 8, 1024), axis=0)

    gain_part = lax.fori_loop(0, 8, du_step, jnp.zeros((8, 1024), F32))
    gp[0, core] = gain_part
    x_g = swap(5, gp.at[0, core], gp.at[0, core])

    for n in range(4):
        at = slice(n * 256, n * 256 + 256)
        dut[at, :] = du[:, at].T

    for n in range(4):
        put_table(n, mm(hot[...], du[:, n * 256 : n * 256 + 256]), 512)
    x_el = swap(6, mp.at[other, :, :, :, :, pl.ds(512, 128)], mr.at[:, :, :, :, pl.ds(512, 128)])

    def proj_step(g, carry):
        rows = pl.ds(pl.multiple_of(g * 256, 256), 256)
        for n in range(2):
            lo, hi = slice(n * 256, n * 256 + 256), slice(512 + n * 256, 768 + n * 256)
            v_lo = mm(dut[rows, :], slot[:, :, lo].reshape(256, 256)).reshape(2, 2, 4, 2, 8, 256)
            v_hi = mm(dut[rows, :], slot[:, :, hi].reshape(256, 256)).reshape(2, 2, 4, 2, 8, 256)
            v = jnp.concatenate([v_lo, v_hi], axis=4).astype(BF)
            for c in range(2):
                for yh in range(2):
                    for yl in range(2):
                        mp[c, g, yh * 2 + yl, :, :, lo] = v[yh, c, :, yl]
        return carry

    lax.fori_loop(0, 4, proj_step, 0)
    x_p = swap(7, mp.at[other, :, :, :, :, pl.ds(0, 512)], mr.at[:, :, :, :, pl.ds(0, 512)])

    for n in range(4):
        at = slice(n * 256, n * 256 + 256)
        gog[:, :, at] = mm_nt(du[...], pw[at, :]).astype(BF).reshape(8, 32, 256)
    own_back = pltpu.make_async_copy(gog.at[tp], gog_o.at[tp], load_sem.at[7])
    own_back.start()
    back = [
        remote(gog.at[(tp + k) % 8], gog_o.at[tp], b_send.at[k - 1], b_recv.at[k - 1], (seq, (tp + k) % 8))
        for k in range(1, 8)
    ]

    x_eg.wait_recv()
    x_el.wait_recv()
    x_p.wait_recv()

    def join_step(i, carry):
        mr[i] = (mr[i].astype(F32) + mp[core, i].astype(F32)).astype(BF)
        return carry

    lax.fori_loop(0, 4, join_step, 0)
    for unit in m_units:
        unit.one.start()
    for copy in back:
        copy.start()

    def gain_swap(step):
        axis = step - 1
        place = spot[axis]
        copies = [
            remote(
                gp.at[step, place],
                gp.at[step, place],
                g_send.at[axis * 3 + k - 1],
                g_recv.at[axis * 3 + k - 1],
                device_at(axis, (place + k) % 4),
            )
            for k in range(1, 4)
        ]
        for copy in copies:
            copy.start()
        return copies

    x_g.wait_recv()
    x_g.wait_send()
    gp[1, x] = gp[0, 0] + gp[0, 1]
    g1 = gain_swap(1)

    for unit in d_units:
        unit.one.finish()
        unit.two.start()
    x_r.wait_recv()
    x_da.wait_recv()
    for unit in m_units:
        unit.one.relay()
    big(dat, dar, r2, upart, u_units)
    for unit in d_units:
        unit.two.relay()

    def gain_join(step, copies):
        for copy in copies:
            copy.wait_recv()
        for copy in copies:
            copy.wait_send()
        return gp[step, 0] + gp[step, 1] + gp[step, 2] + gp[step, 3]

    gp[2, y] = gain_join(1, g1)
    g2 = gain_swap(2)
    for unit in m_units:
        unit.one.finish()
        unit.two.start()
    for unit in d_units:
        unit.two.finish()
        unit.start3()
    for unit in u_units:
        unit.one.relay()
    for unit in m_units:
        unit.two.relay()
    for unit in m_units:
        unit.two.finish()
        unit.start3()
    gp[3, z] = gain_join(2, g2)
    g3 = gain_swap(3)
    for i, unit in enumerate(d_units):
        down_o[:, pl.ds(*cols_of(D_UNITS[i]))] = unit.finish3()
    for unit in u_units:
        unit.one.finish()
        unit.two.start()

    table = m_units[0].finish3()
    agb[core, x, y, z] = table.astype(BF)
    gather = []

    def spread(base, axis, ref):
        copies = [
            remote(ref, ref, q_send.at[base + k - 1], q_recv.at[base + k - 1], device_at(axis, (spot[axis] + k) % 4))
            for k in range(1, 4)
        ]
        for copy in copies:
            copy.start()
        gather.extend(copies)
        return copies

    q1 = spread(0, 2, agb.at[core, x, y, z])
    for i in (1, 2):
        first = M_UNITS[i][0]
        value = m_units[i].finish3()
        proj_o[:, pl.ds(first, 256)] = value[:8]
        proj_o[:, pl.ds(512 + first, 256)] = value[8:]
    for unit in u_units:
        unit.two.relay()
    for copy in q1:
        copy.wait_recv()
    q2 = spread(3, 1, agb.at[core, x, y])
    for unit in u_units:
        unit.two.finish()
        unit.start3()
    for copy in q2:
        copy.wait_recv()
    q3 = spread(6, 0, agb.at[core, x])
    total = gain_join(3, g3)
    gain_o[...] = jnp.sum(total, axis=0, keepdims=True)
    for i, unit in enumerate(u_units):
        up_o[:, pl.ds(*cols_of(U_UNITS[i]))] = unit.finish3()
    for copy in q3:
        copy.wait_recv()
    x_ag = swap(8, agb.at[core], agb.at[core])

    def write_out(c):
        for px in range(4):
            for py in range(4):
                rows = pl.ds(pl.multiple_of(((px * 2 + py // 2) * 2 + c) * 16, 16), 16)
                for pz in range(4):
                    at = (pz * 2 + py % 2) * 128
                    value = agb[c, px, py, pz].astype(F32)
                    embl_o[rows, at : at + 128] = value[:, :128]
                    embg_o[rows, at : at + 128] = value[:, 128:]

    write_out(core)
    x_ag.wait_recv()
    write_out(other)
    for copy in back:
        copy.wait_recv()
    own_back.wait()
    for unit in d_units + m_units + u_units:
        unit.drain()
    for copy in fetch + back + gather + [x_og, x_eg, x_r, x_h, x_da, x_el, x_p, x_ag]:
        copy.wait_send()


def on_device(
    byte_ids,
    global_out,
    global_in_grad,
    out_grad,
    proj_weight,
    emb_local,
    norm_gain,
    up_weight,
    down_weight,
):
    scratch = [pltpu.VMEM(shape, kind) for _, shape, kind in FIXED]
    for _, width, order in ALL_UNITS:
        scratch += unit_scratch(width, order)
    dma = pltpu.SemaphoreType.DMA
    scratch += [dma((8,)), dma((9,)), dma((9,)), dma((7,)), dma((7,)), dma((7,)), dma((7,))]
    scratch += [dma((9, 15)), dma((9, 15)), dma((9,)), dma((9,)), dma((9,)), dma((9,))]
    vmem = pl.BlockSpec(memory_space=pltpu.VMEM)
    anywhere = pl.BlockSpec(memory_space=pl.ANY)
    out = jax.ShapeDtypeStruct
    gog, embg, embl, gain, proj, up, down = pl.pallas_call(
        kernel,
        out_shape=(
            out((8, 32, 1024), BF),
            out((256, 1024), F32),
            out((256, 1024), F32),
            out((1, 1024), F32),
            out((8, 1024), F32),
            out((16, 1024), F32),
            out((16, 1024), F32),
        ),
        in_specs=[vmem] + [anywhere] * 5 + [vmem] + [anywhere] * 2,
        out_specs=[anywhere] + [vmem] * 6,
        scratch_shapes=scratch,
        compiler_params=pltpu.CompilerParams(
            collective_id=0, has_side_effects=True, vmem_limit_bytes=60 * 1024 * 1024
        ),
    )(
        byte_ids.T,
        global_out.reshape(8, 32, 1024),
        global_in_grad,
        out_grad,
        proj_weight,
        emb_local,
        norm_gain.reshape(1, 1024),
        up_weight,
        down_weight,
    )
    return gog.reshape(256, 1024), embg, embl, gain.reshape(1024), proj.T, up.T, down


def solution(mesh):
    placed = (
        P("seq", None),
        P("seq", "tp"),
        P("seq", "tp"),
        P(("seq", "tp"), None),
        P(),
        P(),
        P(),
        P(),
        P(),
    )
    return jax.shard_map(
        on_device,
        mesh=mesh,
        in_specs=placed,
        out_specs=(
            P("seq", "tp"),
            P(),
            P(),
            P(),
            P(None, ("seq", "tp")),
            P(None, ("seq", "tp")),
            P(("seq", "tp"), None),
        ),
        check_vma=False,
    )
```

time: 2160 us -> 91.6 us (0.04)
  waiting for transfers between devices: 2020 us -> 0 us
  Pallas kernels: 0 us -> 81.6 us
  blocking collectives: 67.8 us -> 0 us
  matrix products: 26.1 us -> 0 us
    reduce_scatter x3 -> x0, waiting for transfers between devices: 1950 us -> none  [the longest x1 656 us: on_device(): lax.psum_scatter(up_part, ('seq', 'tp'), scatter_dimension=1, tiled=True)]
    pallas_call x0 -> x1, Pallas kernels: none -> 81.6 us  [on_device(): pl.pallas_call(kernel, out_shape=(out((8, 32, 1024), BF), out((256, 1024)...]
    psum x1 -> x0, blocking collectives: 67.8 us -> none  [on_device(): lax.psum((emb_global_part, emb_local_part, gain_part), ('seq', 'tp'))]
    psum x1 -> x0, waiting for transfers between devices: 62.3 us -> none  [on_device(): lax.psum((emb_global_part, emb_local_part, gain_part), ('seq', 'tp'))]
    dot_general x11 -> x0, matrix products: 26.1 us -> none  [the longest x5 19.8 us: inner(): lax.dot_general(left, right, (((0,), (0,)), ((), ())), preferred_element_...]
  transfers between devices with their start and end apart: 6 -> 0, of which waited for: 5 -> 0; matrix products, arithmetic and copies ran while one was open for 1% -> 0% of each run, Pallas kernels for 0% -> 0%
where the time goes in v1:
time: 91.6 us; the launch traced here: 91.3 us
  Pallas kernels  81.6 us (89%)
  local copies, waits for them, and re-layouts  9 us (10%)
    pallas_call x1, Pallas kernels, on_device(): pl.pallas_call(kernel, out_shape=(out((8, 32, 1024), BF), out((256, 1024)...  81.6 us
    unnamed x15, local copies, waits for them, and re-layouts  9 us

profile of v1, /device:TPU:1, one launch (start us, length us, event | category | flops | bytes accessed | tf_op | source)
XLA Modules:
  0.0 91.3 jit_solution(9396295603592403692)
XLA Ops:
  0.6 81.6 %shard_map.144 = (bf16[8,32,1024]{2,1,0:T(8,128)(2,1)}, f32[256,1024]{1,0:T(8,128)}, f32[256,1024]{1,0:T(8,128)}, f32[1,1024]{1,0:T(1,128)}, f32[8,1024]{1,0:T(8...) custom-call(s32[8,256]{1,0:T(8,128)} %bitcast.11, bf16[8,32,1024]{2,1,0:T(8,128)(2,1)} %bitcast.7, ...), custom_call_target="tpu_custom_call" | custom-call | tf_op jit(solution)/shard_map/pallas_call | solution.py:591
  82.3 0.0 copy-start.3
  82.3 0.0 copy-start.2
  82.3 0.0 copy-start.1
  82.3 0.0 copy-start
  82.3 1.9 %copy.23 = bf16[256,1024]{1,0:T(8,128)(2,1)} copy(bf16[256,1024]{1,0:T(8,128)(2,1)} %bitcast.8) | data formatting | bytes 1048576
  84.2 2.3 %copy.24 = f32[256,1024]{1,0:T(8,128)} copy(f32[256,1024]{1,0:T(8,128)} %get-tuple-element.29) | data formatting | bytes 2097152
  86.5 2.3 %copy.25 = f32[256,1024]{1,0:T(8,128)} copy(f32[256,1024]{1,0:T(8,128)} %get-tuple-element.30) | data formatting | bytes 2097152
  88.8 0.0 copy-done.3
  88.8 0.6 copy.26
  89.4 0.0 copy-done.2
  89.4 0.6 copy.27
  90.0 0.0 copy-done.1
  90.0 0.6 copy.28
  90.7 0.0 copy-done
  90.7 0.6 copy.29
Async XLA Ops:
  82.3 6.6 %copy-start.3 = (f32[1,1024]{1,0:T(1,128)S(1)}, f32[1,1024]{1,0:T(1,128)}, u32[]{:S(2)}) copy-start(f32[1,1024]{1,0:T(1,128)} %get-tuple-element.17) | copy-start | bytes 12292
  82.3 7.1 %copy-start.2 = (f32[8,1024]{1,0:T(8,128)S(1)}, f32[8,1024]{1,0:T(8,128)}, u32[]{:S(2)}) copy-start(f32[8,1024]{1,0:T(8,128)} %get-tuple-element.18) | copy-start | bytes 98308
  82.3 7.8 %copy-start.1 = (f32[16,1024]{1,0:T(8,128)S(1)}, f32[16,1024]{1,0:T(8,128)}, u32[]{:S(2)}) copy-start(f32[16,1024]{1,0:T(8,128)} %get-tuple-element.19) | copy-start | bytes 196612
  82.3 8.4 %copy-start = (f32[16,1024]{1,0:T(8,128)S(1)}, f32[16,1024]{1,0:T(8,128)}, u32[]{:S(2)}) copy-start(f32[16,1024]{1,0:T(8,128)} %get-tuple-element.34) | copy-start | bytes 196612

commit v2 on v1

--- a/solution.py
+++ b/solution.py
@@ -1,5 +1,3 @@
-import functools
-
 import jax
 import jax.numpy as jnp
 from jax import lax
@@ -12,10 +10,10 @@
 MESH = pl.DeviceIdType.MESH
 ALL = slice(None)
 D_UNITS = ((0, 384, (0, 1, 2)), (384, 384, (1, 2, 0)), (768, 256, (2, 0, 1)))
-M_UNITS = ((512, 256, (0, 1, 2)), (0, 256, (1, 2, 0)), (256, 256, (2, 0, 1)))
-U_UNITS = ((0, 256, (0, 1, 2)), (256, 384, (1, 2, 0)), (640, 384, (2, 0, 1)))
-ALL_UNITS = D_UNITS + M_UNITS + U_UNITS
-M_WIDTH = 768
+U_UNITS = ((0, 384, (0, 1, 2)), (384, 256, (1, 2, 0)), (640, 384, (2, 0, 1)))
+P_UNITS = ((0, 256, (0, 1, 2)), (256, 128, (1, 2, 0)), (384, 128, (2, 0, 1)))
+ALL_UNITS = D_UNITS + U_UNITS + P_UNITS
+FAR_FIRST = (2, 1, 3)
 
 
 def mm(a, b):
@@ -139,6 +137,66 @@
         self.two.drain()
         for copy in self.copies:
             copy.wait_send()
+
+
+class Table:
+    def __init__(self, bufs, gathered, spot, core, device_at, partner, send, recv):
+        src, one, two, recv1, recv2, recv3 = bufs
+        self.src, self.out = (src, one, two), (one, two, None)
+        self.recv = (recv1, recv2, recv3)
+        self.spot, self.gathered = spot, gathered
+        x, y, z = spot
+        own = (gathered.at[core, x, y, z], gathered.at[core, x, y], gathered.at[core, x])
+        self.scatter, self.spread = [], []
+        for step in range(3):
+            self.scatter.append(
+                [
+                    remote(
+                        self.src[step].at[(spot[step] + k) % 4],
+                        self.recv[step].at[k - 1],
+                        send.at[step * 3 + k - 1],
+                        recv.at[step * 3 + k - 1],
+                        device_at(step, (spot[step] + k) % 4),
+                    )
+                    for k in FAR_FIRST
+                ]
+            )
+            axis = 2 - step
+            self.spread.append(
+                [
+                    remote(
+                        own[step],
+                        own[step],
+                        send.at[9 + step * 3 + k - 1],
+                        recv.at[9 + step * 3 + k - 1],
+                        device_at(axis, (spot[axis] + k) % 4),
+                    )
+                    for k in FAR_FIRST
+                ]
+            )
+        self.spread.append([remote(gathered.at[core], gathered.at[core], send.at[18], recv.at[18], partner)])
+        self.place = gathered.at[core, x, y, z]
+
+    def start(self, step):
+        for copy in self.scatter[step] if step < 3 else self.spread[step - 3]:
+            copy.start()
+
+    def finish(self, step):
+        for copy in self.scatter[step] if step < 3 else self.spread[step - 3]:
+            copy.wait_recv()
+        if step < 3:
+            total = self.src[step][self.spot[step]].astype(F32)
+            for k in range(3):
+                total = total + self.recv[step][k].astype(F32)
+            if step == 2:
+                self.place[...] = total.astype(BF)
+            else:
+                self.out[step][...] = total.astype(BF)
+
+    def drain(self):
+        for copies in self.scatter + self.spread:
+            for copy in copies:
+                copy.wait_send()
 
 
 def unit_scratch(width, order):
@@ -176,29 +234,43 @@
     ("dut", (1024, 256), BF),
     ("dp", (4, 4, 4, 16, 1024), BF),
     ("upart", (4, 4, 4, 16, 1024), BF),
-    ("mp", (2, 4, 4, 4, 16, M_WIDTH), BF),
-    ("mr", (4, 4, 4, 16, M_WIDTH), BF),
+    ("pp", (2, 4, 4, 4, 16, 512), BF),
+    ("pr", (4, 4, 4, 16, 512), BF),
     ("gog", (8, 32, 1024), BF),
-    ("agb", (2, 4, 4, 4, 16, 256), BF),
-    ("gp", (4, 4, 8, 1024), F32),
+    ("gp", (4, 4, 1, 1024), F32),
 )
+TABLE = (
+    ("part", (2, 4, 4, 4, 16, 128)),
+    ("src", (4, 4, 4, 16, 128)),
+    ("one", (4, 4, 16, 128)),
+    ("two", (4, 16, 128)),
+    ("recv1", (3, 4, 4, 16, 128)),
+    ("recv2", (3, 4, 16, 128)),
+    ("recv3", (3, 16, 128)),
+)
+N_SEMS = {"load": 8, "x": 20, "a": 7, "b": 7, "g": 9, "tg": 19, "tl": 19}
 
 
 def kernel(*refs):
     ids, go_h, gig_h, og_h, pw_h, emb_h, gain, up_h, dn_h = refs[:9]
-    gog_o, embg_o, embl_o, gain_o, proj_o, up_o, down_o = refs[9:16]
+    gog_o, table_g, table_l, gain_o, proj_o, up_o, down_o = refs[9:16]
     rest = list(refs[16:])
     buf = {name: rest.pop(0) for name, _, _ in FIXED}
+    eg = {name: rest.pop(0) for name, _ in TABLE}
+    el = {name: rest.pop(0) for name, _ in TABLE}
     unit_bufs = []
     for _ in ALL_UNITS:
         mine = [rest.pop(0) for _ in range(15)]
         unit_bufs.append((mine[:6], mine[6:12], mine[12], mine[13], mine[14]))
-    load_sem, x_send, x_recv, a_send, a_recv, b_send, b_recv, u_send, u_recv, g_send, g_recv, q_send, q_recv = rest
+    sems = {name: (rest.pop(0), rest.pop(0)) for name in N_SEMS}
+    u_send, u_recv = rest
+    load_sem = sems["load"][0]
+    (x_send, x_recv), (a_send, a_recv), (b_send, b_recv), (g_send, g_recv) = (sems[n] for n in ("x", "a", "b", "g"))
     og, dn, gig, pw, emb, up = (buf[n] for n in ("og", "dn", "gig", "pw", "emb", "up"))
     og2, slot, dh, norm, scale, r2 = (buf[n] for n in ("og2", "slot", "dh", "norm", "scale", "r2"))
     hot, ht, hr, dat, dar, da = (buf[n] for n in ("hot", "ht", "hr", "dat", "dar", "da"))
-    dr, du, dut, dp, upart, mp = (buf[n] for n in ("dr", "du", "dut", "dp", "upart", "mp"))
-    mr, gog, agb, gp = (buf[n] for n in ("mr", "gog", "agb", "gp"))
+    dr, du, dut, dp, upart, pp = (buf[n] for n in ("dr", "du", "dut", "dp", "upart", "pp"))
+    pr, gog, gp = (buf[n] for n in ("pr", "gog", "gp"))
 
     seq = lax.axis_index("seq")
     tp = lax.axis_index("tp")
@@ -281,21 +353,37 @@
     prev_id = jnp.where(iota((1, 256), 1) < 32, -1, prev.astype(jnp.int32))
     hot[...] = (row == prev_id).astype(BF)
 
-    def put_table(n, value, first):
+    def table_of(bufs, gathered, name):
+        order = tuple(bufs[n] for n in ("src", "one", "two", "recv1", "recv2", "recv3"))
+        return Table(order, gathered, spot, core, device_at, partner, *sems[name])
+
+    glob, loc = table_of(eg, table_g, "tg"), table_of(el, table_l, "tl")
+
+    def put_table(part, n, value):
         block = value.astype(BF).reshape(4, 2, 2, 16, 256)
         for c in range(2):
             for yh in range(2):
                 for yl in range(2):
-                    mp[c, :, yh * 2 + yl, n, :, pl.ds(first, 128)] = block[:, yh, c, :, yl * 128 : yl * 128 + 128]
+                    part[c, :, yh * 2 + yl, n] = block[:, yh, c, :, yl * 128 : yl * 128 + 128]
+
+    def join(part, src):
+        def step(i, carry):
+            src[i] = (src[i].astype(F32) + part[core, i].astype(F32)).astype(BF)
+            return carry
+
+        lax.fori_loop(0, 4, step, 0)
 
     loads["gig"].wait()
     for n in range(4):
-        put_table(n, mm(hot_own, gig[:, n * 256 : n * 256 + 256]), 640)
-    x_eg = swap(1, mp.at[other, :, :, :, :, pl.ds(640, 128)], mr.at[:, :, :, :, pl.ds(640, 128)])
+        put_table(eg["part"], n, mm(hot_own, gig[:, n * 256 : n * 256 + 256]))
+    x_eg = swap(1, eg["part"].at[other], eg["src"])
 
     loads["pw"].wait()
     loads["emb"].wait()
     loads["own"].wait()
+    x_eg.wait_recv()
+    join(eg["part"], eg["src"])
+    glob.start(0)
     for copy in fetch:
         copy.wait_recv()
 
@@ -316,69 +404,80 @@
     x_r = swap(2, r2.at[0], r2.at[1])
 
     loads["up"].wait()
-
-    def ff_step(k, carry):
-        at = pl.ds(pl.multiple_of(k * 256, 256), 256)
-        rows = pl.ds(pl.multiple_of(k * 128, 128), 128)
-        a = mm(r2[0], up[:, at])
-        sig = jax.nn.sigmoid(a)
-        h_t = (a * sig).astype(BF).T
-        ht[0, rows, :] = h_t[:128]
-        ht[1, rows, :] = h_t[128:]
-        da_v = (dh[k] * sig * (1.0 + a * (1.0 - sig))).astype(BF)
-        da[:, at] = da_v
-        da_t = da_v.T
-        dat[0, rows, :] = da_t[:128]
-        dat[1, rows, :] = da_t[128:]
+    glob.finish(0)
+    glob.start(1)
+
+    def h_swap(j):
+        rows = pl.ds(pl.multiple_of(j * 256, 256), 256)
+        return remote(ht.at[other, rows], hr.at[rows], x_send.at[8 + j], x_recv.at[8 + j], partner)
+
+    def ff_step(j, carry):
+        for k2 in range(2):
+            k = j * 2 + k2
+            at = pl.ds(pl.multiple_of(k * 256, 256), 256)
+            rows = pl.ds(pl.multiple_of(k * 128, 128), 128)
+            a = mm(r2[0], up[:, at])
+            sig = jax.nn.sigmoid(a)
+            h_t = (a * sig).astype(BF).T
+            ht[0, rows, :] = h_t[:128]
+            ht[1, rows, :] = h_t[128:]
+            da_v = (dh[k] * sig * (1.0 + a * (1.0 - sig))).astype(BF)
+            da[:, at] = da_v
+            da_t = da_v.T
+            dat[0, rows, :] = da_t[:128]
+            dat[1, rows, :] = da_t[128:]
+        h_swap(j).start()
         return carry
 
-    lax.fori_loop(0, 8, ff_step, 0)
-    x_h = swap(3, ht.at[other], hr)
-    x_da = swap(4, dat.at[other], dar)
+    lax.fori_loop(0, 2, ff_step, 0)
+    glob.finish(1)
+    glob.start(2)
+    lax.fori_loop(2, 4, ff_step, 0)
 
     def units(src, table, first):
         return [
-            Unit(src, cols_of(t), t[2], spot, device_at, unit_bufs[first + i], u_send.at[first + i], u_recv.at[first + i])
+            Unit(src, t[:2], t[2], spot, device_at, unit_bufs[first + i], u_send.at[first + i], u_recv.at[first + i])
             for i, t in enumerate(table)
         ]
 
-    def cols_of(entry):
-        return entry[0], entry[1]
-
     d_units = units(dp, D_UNITS, 0)
-    m_units = units(mr, M_UNITS, 3)
-    u_units = units(upart, U_UNITS, 6)
-
-    def big(lhs, lhs_far, rhs, out, table):
-        done = 0
-        for n in range(4):
-            at = slice(n * 256, n * 256 + 256)
-
-            def step(g, carry):
-                rows = pl.ds(pl.multiple_of(g * 512, 512), 512)
-                v = mm(lhs[core, rows, :], rhs[0, :, at]) + mm(lhs_far[rows, :], rhs[1, :, at])
-                v = v.astype(BF).reshape(2, 2, 4, 2, 16, 256)
-                for xx in range(2):
-                    for yh in range(2):
-                        for yl in range(2):
-                            out[2 * g + xx, yh * 2 + yl, :, :, at] = v[xx, yh, :, yl]
-                return carry
-
-            lax.fori_loop(0, 2, step, 0)
-            while done < 3 and table[done].one.cols[0] + table[done].one.cols[1] <= n * 256 + 256:
-                table[done].one.start()
-                done += 1
+    u_units = units(upart, U_UNITS, 3)
+    p_units = units(pr, P_UNITS, 6)
+
+    def big(lhs, lhs_far, rhs, out, n):
+        at = slice(n * 256, n * 256 + 256)
+
+        def step(g, carry):
+            rows = pl.ds(pl.multiple_of(g * 512, 512), 512)
+            v = mm(lhs[core, rows, :], rhs[0, :, at]) + mm(lhs_far[rows, :], rhs[1, :, at])
+            v = v.astype(BF).reshape(2, 2, 4, 2, 16, 256)
+            for xx in range(2):
+                for yh in range(2):
+                    for yl in range(2):
+                        out[2 * g + xx, yh * 2 + yl, :, :, at] = v[xx, yh, :, yl]
+            return carry
+
+        lax.fori_loop(0, 2, step, 0)
 
     x_og.wait_recv()
-    x_h.wait_recv()
-    big(ht, hr, og2, dp, d_units)
+    for j in range(4):
+        h_swap(j).wait_recv()
+    x_da = swap(4, dat.at[other], dar)
+    big(ht, hr, og2, dp, 0)
+    glob.finish(2)
+    glob.start(3)
+    big(ht, hr, og2, dp, 1)
+    d_units[0].one.start()
+    big(ht, hr, og2, dp, 2)
+    d_units[1].one.start()
+    big(ht, hr, og2, dp, 3)
+    d_units[2].one.start()
 
     for n in range(4):
         at = slice(n * 256, n * 256 + 256)
         dr[:, at] = mm_nt(da[...], up[at, :])
-    for unit in d_units:
-        unit.one.relay()
-
+    glob.finish(3)
+    glob.start(4)
     gain_v = gain[...]
 
     def du_step(i, total):
@@ -393,56 +492,31 @@
         return total + jnp.sum(product.reshape(4, 8, 1024), axis=0)
 
     gain_part = lax.fori_loop(0, 8, du_step, jnp.zeros((8, 1024), F32))
-    gp[0, core] = gain_part
+    gp[0, core] = jnp.sum(gain_part, axis=0, keepdims=True)
     x_g = swap(5, gp.at[0, core], gp.at[0, core])
-
+    for n in range(4):
+        put_table(el["part"], n, mm(hot[...], du[:, n * 256 : n * 256 + 256]))
+    x_el = swap(6, el["part"].at[other], el["src"])
+    for unit in d_units:
+        unit.one.relay()
     for n in range(4):
         at = slice(n * 256, n * 256 + 256)
         dut[at, :] = du[:, at].T
-
-    for n in range(4):
-        put_table(n, mm(hot[...], du[:, n * 256 : n * 256 + 256]), 512)
-    x_el = swap(6, mp.at[other, :, :, :, :, pl.ds(512, 128)], mr.at[:, :, :, :, pl.ds(512, 128)])
-
-    def proj_step(g, carry):
-        rows = pl.ds(pl.multiple_of(g * 256, 256), 256)
-        for n in range(2):
-            lo, hi = slice(n * 256, n * 256 + 256), slice(512 + n * 256, 768 + n * 256)
-            v_lo = mm(dut[rows, :], slot[:, :, lo].reshape(256, 256)).reshape(2, 2, 4, 2, 8, 256)
-            v_hi = mm(dut[rows, :], slot[:, :, hi].reshape(256, 256)).reshape(2, 2, 4, 2, 8, 256)
-            v = jnp.concatenate([v_lo, v_hi], axis=4).astype(BF)
-            for c in range(2):
-                for yh in range(2):
-                    for yl in range(2):
-                        mp[c, g, yh * 2 + yl, :, :, lo] = v[yh, c, :, yl]
-        return carry
-
-    lax.fori_loop(0, 4, proj_step, 0)
-    x_p = swap(7, mp.at[other, :, :, :, :, pl.ds(0, 512)], mr.at[:, :, :, :, pl.ds(0, 512)])
-
-    for n in range(4):
-        at = slice(n * 256, n * 256 + 256)
-        gog[:, :, at] = mm_nt(du[...], pw[at, :]).astype(BF).reshape(8, 32, 256)
-    own_back = pltpu.make_async_copy(gog.at[tp], gog_o.at[tp], load_sem.at[7])
-    own_back.start()
-    back = [
-        remote(gog.at[(tp + k) % 8], gog_o.at[tp], b_send.at[k - 1], b_recv.at[k - 1], (seq, (tp + k) % 8))
-        for k in range(1, 8)
-    ]
-
-    x_eg.wait_recv()
+    glob.finish(4)
+    glob.start(5)
+
+    x_r.wait_recv()
+    x_da.wait_recv()
+    big(dat, dar, r2, upart, 0)
     x_el.wait_recv()
-    x_p.wait_recv()
-
-    def join_step(i, carry):
-        mr[i] = (mr[i].astype(F32) + mp[core, i].astype(F32)).astype(BF)
-        return carry
-
-    lax.fori_loop(0, 4, join_step, 0)
-    for unit in m_units:
-        unit.one.start()
-    for copy in back:
-        copy.start()
+    join(el["part"], el["src"])
+    loc.start(0)
+    big(dat, dar, r2, upart, 1)
+    u_units[0].one.start()
+    big(dat, dar, r2, upart, 2)
+    u_units[1].one.start()
+    big(dat, dar, r2, upart, 3)
+    u_units[2].one.start()
 
     def gain_swap(step):
         axis = step - 1
@@ -455,27 +529,11 @@
                 g_recv.at[axis * 3 + k - 1],
                 device_at(axis, (place + k) % 4),
             )
-            for k in range(1, 4)
+            for k in FAR_FIRST
         ]
         for copy in copies:
             copy.start()
         return copies
-
-    x_g.wait_recv()
-    x_g.wait_send()
-    gp[1, x] = gp[0, 0] + gp[0, 1]
-    g1 = gain_swap(1)
-
-    for unit in d_units:
-        unit.one.finish()
-        unit.two.start()
-    x_r.wait_recv()
-    x_da.wait_recv()
-    for unit in m_units:
-        unit.one.relay()
-    big(dat, dar, r2, upart, u_units)
-    for unit in d_units:
-        unit.two.relay()
 
     def gain_join(step, copies):
         for copy in copies:
@@ -484,88 +542,126 @@
             copy.wait_send()
         return gp[step, 0] + gp[step, 1] + gp[step, 2] + gp[step, 3]
 
+    x_g.wait_recv()
+    x_g.wait_send()
+    gp[1, x] = gp[0, 0] + gp[0, 1]
+    g1 = gain_swap(1)
+    for unit in d_units:
+        unit.one.finish()
+        unit.two.start()
+
+    def proj_step(g, carry):
+        rows = pl.ds(pl.multiple_of(g * 256, 256), 256)
+        for n in range(2):
+            lo, hi = slice(n * 256, n * 256 + 256), slice(512 + n * 256, 768 + n * 256)
+            v_lo = mm(dut[rows, :], slot[:, :, lo].reshape(256, 256)).reshape(2, 2, 4, 2, 8, 256)
+            v_hi = mm(dut[rows, :], slot[:, :, hi].reshape(256, 256)).reshape(2, 2, 4, 2, 8, 256)
+            v = jnp.concatenate([v_lo, v_hi], axis=4).astype(BF)
+            for c in range(2):
+                for yh in range(2):
+                    for yl in range(2):
+                        pp[c, g, yh * 2 + yl, :, :, lo] = v[yh, c, :, yl]
+        return carry
+
+    lax.fori_loop(0, 4, proj_step, 0)
+    x_p = swap(7, pp.at[other], pr)
+    loc.finish(0)
+    loc.start(1)
+    glob.finish(5)
+    glob.start(6)
+    for n in range(4):
+        at = slice(n * 256, n * 256 + 256)
+        gog[:, :, at] = mm_nt(du[...], pw[at, :]).astype(BF).reshape(8, 32, 256)
+    own_back = pltpu.make_async_copy(gog.at[tp], gog_o.at[tp], load_sem.at[7])
+    own_back.start()
+    back = [
+        remote(gog.at[(tp + k) % 8], gog_o.at[tp], b_send.at[k - 1], b_recv.at[k - 1], (seq, (tp + k) % 8))
+        for k in range(1, 8)
+    ]
+    x_p.wait_recv()
+    join(pp, pr)
+    for unit in p_units:
+        unit.one.start()
+    for unit in u_units:
+        unit.one.relay()
     gp[2, y] = gain_join(1, g1)
     g2 = gain_swap(2)
-    for unit in m_units:
+    loc.finish(1)
+    loc.start(2)
+    for unit in d_units:
+        unit.two.relay()
+    for unit in p_units:
+        unit.one.relay()
+    loc.finish(2)
+    loc.start(3)
+    for unit in u_units:
         unit.one.finish()
         unit.two.start()
+    gp[3, z] = gain_join(2, g2)
+    g3 = gain_swap(3)
     for unit in d_units:
         unit.two.finish()
         unit.start3()
-    for unit in u_units:
-        unit.one.relay()
-    for unit in m_units:
-        unit.two.relay()
-    for unit in m_units:
-        unit.two.finish()
-        unit.start3()
-    gp[3, z] = gain_join(2, g2)
-    g3 = gain_swap(3)
-    for i, unit in enumerate(d_units):
-        down_o[:, pl.ds(*cols_of(D_UNITS[i]))] = unit.finish3()
-    for unit in u_units:
+    loc.finish(3)
+    loc.start(4)
+    for unit in p_units:
         unit.one.finish()
         unit.two.start()
-
-    table = m_units[0].finish3()
-    agb[core, x, y, z] = table.astype(BF)
-    gather = []
-
-    def spread(base, axis, ref):
-        copies = [
-            remote(ref, ref, q_send.at[base + k - 1], q_recv.at[base + k - 1], device_at(axis, (spot[axis] + k) % 4))
-            for k in range(1, 4)
-        ]
-        for copy in copies:
-            copy.start()
-        gather.extend(copies)
-        return copies
-
-    q1 = spread(0, 2, agb.at[core, x, y, z])
-    for i in (1, 2):
-        first = M_UNITS[i][0]
-        value = m_units[i].finish3()
-        proj_o[:, pl.ds(first, 256)] = value[:8]
-        proj_o[:, pl.ds(512 + first, 256)] = value[8:]
+    for copy in back:
+        copy.start()
     for unit in u_units:
         unit.two.relay()
-    for copy in q1:
-        copy.wait_recv()
-    q2 = spread(3, 1, agb.at[core, x, y])
+    loc.finish(4)
+    loc.start(5)
+    for unit in p_units:
+        unit.two.relay()
+    for i, unit in enumerate(d_units):
+        down_o[:, pl.ds(*D_UNITS[i][:2])] = unit.finish3()
     for unit in u_units:
         unit.two.finish()
         unit.start3()
-    for copy in q2:
-        copy.wait_recv()
-    q3 = spread(6, 0, agb.at[core, x])
-    total = gain_join(3, g3)
-    gain_o[...] = jnp.sum(total, axis=0, keepdims=True)
+    for unit in p_units:
+        unit.two.finish()
+        unit.start3()
+    gain_o[...] = gain_join(3, g3)
+    loc.finish(5)
+    loc.start(6)
     for i, unit in enumerate(u_units):
-        up_o[:, pl.ds(*cols_of(U_UNITS[i]))] = unit.finish3()
-    for copy in q3:
-        copy.wait_recv()
-    x_ag = swap(8, agb.at[core], agb.at[core])
-
-    def write_out(c):
-        for px in range(4):
-            for py in range(4):
-                rows = pl.ds(pl.multiple_of(((px * 2 + py // 2) * 2 + c) * 16, 16), 16)
-                for pz in range(4):
-                    at = (pz * 2 + py % 2) * 128
-                    value = agb[c, px, py, pz].astype(F32)
-                    embl_o[rows, at : at + 128] = value[:, :128]
-                    embg_o[rows, at : at + 128] = value[:, 128:]
-
-    write_out(core)
-    x_ag.wait_recv()
-    write_out(other)
+        up_o[:, pl.ds(*U_UNITS[i][:2])] = unit.finish3()
+    for i, unit in enumerate(p_units):
+        first, width, _ = P_UNITS[i]
+        value = unit.finish3()
+        proj_o[:, pl.ds(first, width)] = value[:8]
+        proj_o[:, pl.ds(512 + first, width)] = value[8:]
+    glob.finish(6)
     for copy in back:
         copy.wait_recv()
     own_back.wait()
-    for unit in d_units + m_units + u_units:
+    loc.finish(6)
+    glob.drain()
+    loc.drain()
+    for unit in d_units + u_units + p_units:
         unit.drain()
-    for copy in fetch + back + gather + [x_og, x_eg, x_r, x_h, x_da, x_el, x_p, x_ag]:
+    for copy in fetch + back + [x_og, x_eg, x_r, x_da, x_el, x_p] + [h_swap(j) for j in range(4)]:
         copy.wait_send()
+
+
+def finish(gog, table_g, table_l, gain, proj, up, down, gog_o, embg_o, embl_o, gain_o, proj_o, up_o, down_o, embg, embl, sem):
+    pairs = ((gog, gog_o), (gain, gain_o), (proj, proj_o), (up, up_o), (down, down_o))
+    copies = [pltpu.make_async_copy(src, dst, sem.at[n]) for n, (src, dst) in enumerate(pairs)]
+    for copy in copies:
+        copy.start()
+    for n, (table, value, out) in enumerate(((table_g, embg, embg_o), (table_l, embl, embl_o))):
+        for row in range(16):
+            px, yh, c = row // 4, row // 2 % 2, row % 2
+            for col in range(8):
+                pz, yl = col // 2, col % 2
+                value[row * 16 : row * 16 + 16, col * 128 : col * 128 + 128] = table[c, px, yh * 2 + yl, pz].astype(F32)
+        copy = pltpu.make_async_copy(value, out, sem.at[5 + n])
+        copy.start()
+        copies.append(copy)
+    for copy in copies:
+        copy.wait()
 
 
 def on_device(
@@ -580,30 +676,31 @@
     down_weight,
 ):
     scratch = [pltpu.VMEM(shape, kind) for _, shape, kind in FIXED]
+    scratch += [pltpu.VMEM(shape, BF) for _, shape in TABLE] * 2
     for _, width, order in ALL_UNITS:
         scratch += unit_scratch(width, order)
     dma = pltpu.SemaphoreType.DMA
-    scratch += [dma((8,)), dma((9,)), dma((9,)), dma((7,)), dma((7,)), dma((7,)), dma((7,))]
-    scratch += [dma((9, 15)), dma((9, 15)), dma((9,)), dma((9,)), dma((9,)), dma((9,))]
+    for count in N_SEMS.values():
+        scratch += [dma((count,)), dma((count,))]
+    scratch += [dma((9, 15)), dma((9, 15))]
     vmem = pl.BlockSpec(memory_space=pltpu.VMEM)
     anywhere = pl.BlockSpec(memory_space=pl.ANY)
-    out = jax.ShapeDtypeStruct
-    gog, embg, embl, gain, proj, up, down = pl.pallas_call(
+    parts = pl.pallas_call(
         kernel,
         out_shape=(
-            out((8, 32, 1024), BF),
-            out((256, 1024), F32),
-            out((256, 1024), F32),
-            out((1, 1024), F32),
-            out((8, 1024), F32),
-            out((16, 1024), F32),
-            out((16, 1024), F32),
+            pltpu.VMEM((8, 32, 1024), BF),
+            pltpu.VMEM((2, 4, 4, 4, 16, 128), BF),
+            pltpu.VMEM((2, 4, 4, 4, 16, 128), BF),
+            pltpu.VMEM((1, 1024), F32),
+            pltpu.VMEM((8, 1024), F32),
+            pltpu.VMEM((16, 1024), F32),
+            pltpu.VMEM((16, 1024), F32),
         ),
         in_specs=[vmem] + [anywhere] * 5 + [vmem] + [anywhere] * 2,
-        out_specs=[anywhere] + [vmem] * 6,
+        out_specs=[vmem] * 7,
         scratch_shapes=scratch,
         compiler_params=pltpu.CompilerParams(
-            collective_id=0, has_side_effects=True, vmem_limit_bytes=60 * 1024 * 1024
+            collective_id=0, has_side_effects=True, vmem_limit_bytes=52 * 1024 * 1024
         ),
     )(
         byte_ids.T,
@@ -616,6 +713,23 @@
         up_weight,
         down_weight,
     )
+    out = jax.ShapeDtypeStruct
+    gog, embg, embl, gain, proj, up, down = pl.pallas_call(
+        finish,
+        out_shape=(
+            out((8, 32, 1024), BF),
+            out((256, 1024), F32),
+            out((256, 1024), F32),
+            out((1, 1024), F32),
+            out((8, 1024), F32),
+            out((16, 1024), F32),
+            out((16, 1024), F32),
+        ),
+        in_specs=[vmem] * 7,
+        out_specs=[anywhere] * 7,
+        scratch_shapes=[pltpu.VMEM((256, 1024), F32), pltpu.VMEM((256, 1024), F32), dma((7,))],
+        compiler_params=pltpu.CompilerParams(vmem_limit_bytes=6 * 1024 * 1024),
+    )(*parts)
     return gog.reshape(256, 1024), embg, embl, gain.reshape(1024), proj.T, up.T, down
 
 

time: 91.6 us -> 73.5 us (0.80)
  Pallas kernels: 81.6 us -> 70.9 us
  local copies, waits for them, and re-layouts: 9 us -> 1.38 us
    pallas_call x1 -> x2, Pallas kernels: 81.6 us -> 70.9 us  [the longest x1 69.3 us: on_device(): pl.pallas_call(kernel, out_shape=(pltpu.VMEM((8, 32, 1024), BF), pltpu.VM...]
    unnamed x15 -> x4, local copies, waits for them, and re-layouts: 9 us -> 1.38 us
where the time goes in v2:
time: 73.5 us; the launch traced here: 73 us
  Pallas kernels  70.9 us (96%)
  local copies, waits for them, and re-layouts  1.38 us (2%)
    pallas_call x1, Pallas kernels, on_device(): pl.pallas_call(kernel, out_shape=(pltpu.VMEM((8, 32, 1024), BF), pltpu.VM...  69.3 us
    pallas_call x1, Pallas kernels, on_device(): pl.pallas_call(finish, out_shape=(out((8, 32, 1024), BF), out((256, 1024)...  1.61 us

profile of v2, /device:TPU:1, one launch (start us, length us, event | category | flops | bytes accessed | tf_op | source)
XLA Modules:
  0.0 73.0 jit_solution(10225276216382518305)
XLA Ops:
  0.6 0.0 copy-start
  0.6 0.7 copy-done
  1.3 0.0 copy-start.1
  1.3 0.7 copy-done.1
  2.0 69.3 %shard_map.144 = (bf16[8,32,1024]{2,1,0:T(8,128)(2,1)S(1)}, bf16[2,4,4,4,16,128]{5,4,3,2,1,0:T(8,128)(2,1)S(1)}, bf16[2,4,4,4,16,128]{5,4,3,2,1,0:T(8,128)(2,1)S...) custom-call(s32[8,256]{1,0:T(8,128)S(1)} %bitcast.7, ...), custom_call_target="tpu_custom_call" | custom-call | tf_op jit(solution)/shard_map/pallas_call | solution.py:688
  71.3 1.6 %shard_map.145 = (bf16[8,32,1024]{2,1,0:T(8,128)(2,1)}, f32[256,1024]{1,0:T(8,128)}, f32[256,1024]{1,0:T(8,128)}, f32[1,1024]{1,0:T(1,128)}, f32[8,1024]{1,0:T(8...) custom-call(bf16[8,32,1024]{2,1,0:T(8,128)(2,1)S(1)} %get-tuple-element.21.gog, ...), custom_call_target="tpu_custom_call" | custom-call | tf_op jit(solution)/shard_map/pallas_call | solution.py:717
Async XLA Ops:
  0.6 0.7 copy-start
  1.3 0.7 copy-start.1

commit v3 on v2

v3 whole, which is shorter than its diff:
```python
import jax
import jax.numpy as jnp
from jax import lax
from jax.experimental import pallas as pl
from jax.experimental.pallas import tpu as pltpu
from jax.sharding import PartitionSpec as P

BF = jnp.bfloat16
F32 = jnp.float32
MESH = pl.DeviceIdType.MESH
ALL = slice(None)
D_UNITS = ((0, 256, (0, 1, 2)), (256, 384, (1, 2, 0)), (640, 384, (2, 0, 1)))
U_UNITS = ((0, 256, (0, 1, 2)), (256, 384, (1, 2, 0)), (640, 384, (2, 0, 1)))
P_UNITS = ((0, 256, (0, 1, 2)), (256, 128, (1, 2, 0)), (384, 128, (2, 0, 1)))
ALL_UNITS = D_UNITS + U_UNITS + P_UNITS
FAR_FIRST = (2, 1, 3)
PLANE = tuple((ky, kz) for ky in (2, 1, 3, 0) for kz in (2, 1, 3, 0) if ky or kz)


def mm(a, b):
    return lax.dot_general(a, b, (((1,), (0,)), ((), ())), preferred_element_type=F32)


def mm_nt(a, b):
    return lax.dot_general(a, b, (((1,), (1,)), ((), ())), preferred_element_type=F32)


def mm_tn(a, b):
    return lax.dot_general(a, b, (((0,), (0,)), ((), ())), preferred_element_type=F32)


def iota(shape, dim):
    return lax.broadcasted_iota(jnp.int32, shape, dim)


def remote(src, dst, send, recv, device):
    return pltpu.make_async_remote_copy(
        src_ref=src, dst_ref=dst, send_sem=send, recv_sem=recv, device_id=device, device_id_type=MESH
    )


def await_recv(ref, sem, device):
    remote(ref, ref, sem, sem, device).wait_recv()


def await_send(ref, sem, device):
    remote(ref, ref, sem, sem, device).wait_send()


class Ring:
    def __init__(self, src, cols, over, half, spot, device_at, buf, out, send, recv):
        self.src, self.cols, self.over, self.half = src, cols, over, half
        self.buf, self.out, self.send, self.recv = buf, out, send, recv
        here = spot[over]
        self.here, self.right, self.left, self.far = here, (here + 1) % 4, (here + 3) % 4, (here + 2) % 4
        self.to_right = device_at(over, self.right)
        self.to_left = device_at(over, self.left)

    def part(self, place, half):
        index = tuple(
            place if a == self.over else pl.ds(2 * half, 2) if a == self.half else ALL for a in (0, 1, 2)
        )
        return self.src.at[index + (ALL, pl.ds(*self.cols))]

    def start(self):
        for src, n, sem, device in (
            (self.part(self.far, 0), 0, 0, self.to_right),
            (self.part(self.far, 1), 1, 0, self.to_left),
            (self.part(self.right, 1), 2, 1, self.to_right),
            (self.part(self.left, 0), 3, 1, self.to_left),
        ):
            remote(src, self.buf.at[n], self.send, self.recv[sem], device).start()

    def relay(self):
        await_recv(self.buf.at[pl.ds(0, 2)], self.recv[0], self.to_left)
        self.buf[0] = (self.buf[0].astype(F32) + self.part(self.right, 0)[...].astype(F32)).astype(BF)
        remote(self.buf.at[0], self.buf.at[4], self.send, self.recv[1], self.to_right).start()
        self.buf[1] = (self.buf[1].astype(F32) + self.part(self.left, 1)[...].astype(F32)).astype(BF)
        remote(self.buf.at[1], self.buf.at[5], self.send, self.recv[1], self.to_left).start()

    def out_half(self, half):
        index = tuple(pl.ds(2 * half, 2) if a == self.half else ALL for a in (0, 1, 2) if a != self.over)
        return self.out.at[index]

    def finish(self):
        await_recv(self.buf.at[pl.ds(2, 4)], self.recv[1], self.to_left)
        for half in range(2):
            self.out_half(half)[...] = (
                self.part(self.here, half)[...].astype(F32)
                + self.buf[4 + half].astype(F32)
                + self.buf[3 - half].astype(F32)
            ).astype(BF)

    def drain(self):
        await_send(self.buf, self.send, self.to_left)


class Direct:
    def __init__(self, src, axes, over, spot, device_at, buf, send, recv):
        self.src, self.axes, self.over, self.buf, self.send, self.recv = src, axes, over, buf, send, recv
        self.here = spot[over]
        self.device_at = device_at

    def part(self, place):
        return self.src.at[tuple(place if a == self.over else ALL for a in self.axes)]

    def start(self):
        for k in FAR_FIRST:
            there = (self.here + k) % 4
            self.to = self.device_at(self.over, there)
            remote(self.part(there), self.buf.at[k - 1], self.send, self.recv, self.to).start()

    def finish(self):
        await_recv(self.buf, self.recv, self.to)
        total = self.part(self.here)[...].astype(F32)
        for k in range(3):
            total = total + self.buf[k].astype(F32)
        return total

    def drain(self):
        await_send(self.buf, self.send, self.to)


class Unit:
    def __init__(self, src, cols, order, spot, device_at, bufs, sems):
        a, b, c = order
        first, out1, second, self.out2, last = bufs
        rest = tuple(n for n in (0, 1, 2) if n != a)
        self.one = Ring(src, cols, a, b, spot, device_at, first, out1, sems.at[0], (sems.at[1], sems.at[2]))
        self.two = Direct(out1, rest, b, spot, device_at, second, sems.at[3], sems.at[4])
        self.three = Direct(self.out2, (c,), c, spot, device_at, last, sems.at[5], sems.at[6])

    def start2(self):
        self.one.finish()
        self.two.start()

    def start3(self):
        self.out2[...] = self.two.finish().astype(BF)
        self.three.start()

    def drain(self):
        self.one.drain()
        self.two.drain()
        self.three.drain()


class Table:
    def __init__(self, bufs, gathered, spot, core, device, device_at, partner, sems):
        src, self.one, recv1, self.recv2 = bufs
        self.partner, self.sems = partner, sems
        x, y, z = spot
        self.spot = spot
        self.first = Direct(src, (0, 1, 2), 0, spot, device_at, recv1, sems.at[0], sems.at[1])
        self.own = (gathered.at[core, x, y, z], gathered.at[core, x], gathered.at[core])
        self.sized = (self.recv2, recv1, gathered.at[core])
        self.plane = []
        for ky, kz in PLANE:
            py, pz = (y + ky) % 4, (z + kz) % 4
            self.plane.append((py, pz, ky * 4 + kz - 1, device(x, py, pz, core)))
        self.to = (
            [there for _, _, _, there in self.plane],
            [device_at(0, (x + k) % 4) for k in FAR_FIRST],
            [partner],
        )

    def start(self, step):
        send, recv = self.sems.at[2 * step], self.sems.at[2 * step + 1]
        if step == 0:
            self.first.start()
        elif step == 1:
            for py, pz, n, there in self.plane:
                remote(self.one.at[py, pz], self.recv2.at[n], send, recv, there).start()
        else:
            n = step - 2
            for there in self.to[n]:
                remote(self.own[n], self.own[n], send, recv, there).start()

    def finish(self, step):
        if step == 0:
            self.one[...] = self.first.finish().astype(BF)
            return
        await_recv(self.recv2 if step == 1 else self.sized[step - 2], self.sems.at[2 * step + 1], self.partner)
        if step == 1:
            total = self.one[self.spot[1], self.spot[2]].astype(F32)
            for n in range(15):
                total = total + self.recv2[n].astype(F32)
            self.own[0][...] = total.astype(BF)

    def drain(self):
        self.first.drain()
        await_send(self.recv2, self.sems.at[2], self.partner)
        for n in range(3):
            await_send(self.sized[n], self.sems.at[2 * n + 4], self.partner)


def unit_scratch(width, order):
    a, b, c = order
    rest = tuple(n for n in (0, 1, 2) if n != a)
    one = tuple(2 if n == b else 4 for n in rest)
    return [
        pltpu.VMEM((6,) + one + (16, width), BF),
        pltpu.VMEM((4, 4, 16, width), BF),
        pltpu.VMEM((3, 4, 16, width), BF),
        pltpu.VMEM((4, 16, width), BF),
        pltpu.VMEM((3, 16, width), BF),
    ]


FIXED = (
    ("ids", (8, 256), jnp.int32),
    ("gain", (1, 1024), F32),
    ("og", (256, 1024), BF),
    ("dn", (2048, 1024), BF),
    ("gig", (256, 1024), BF),
    ("pw", (1024, 1024), BF),
    ("emb", (256, 1024), BF),
    ("up", (1024, 2048), BF),
    ("og2", (512, 1024), BF),
    ("slot", (8, 32, 1024), BF),
    ("dh", (8, 256, 256), F32),
    ("norm", (256, 1024), F32),
    ("scale", (256, 128), F32),
    ("r2", (512, 1024), BF),
    ("hot", (256, 256), BF),
    ("ht", (2, 1024, 512), BF),
    ("dat", (2, 1024, 512), BF),
    ("da", (256, 2048), BF),
    ("dr", (256, 1024), F32),
    ("du", (256, 1024), BF),
    ("dut", (1024, 256), BF),
    ("dp", (4, 4, 4, 16, 1024), BF),
    ("upart", (4, 4, 4, 16, 1024), BF),
    ("pp", (2, 4, 4, 4, 16, 512), BF),
    ("pr", (4, 4, 4, 16, 512), BF),
    ("gog", (8, 32, 1024), BF),
    ("gp", (4, 4, 1, 1024), F32),
)
TABLE = (
    ("part", (2, 4, 4, 4, 16, 128)),
    ("src", (4, 4, 4, 16, 128)),
    ("one", (4, 4, 16, 128)),
    ("recv1", (3, 4, 4, 16, 128)),
    ("recv2", (15, 16, 128)),
)
N_LOADS, N_X = 10, 14


def kernel(*refs):
    ids_h, go_h, gig_h, og_h, pw_h, emb_h, gain_h, up_h, dn_h = refs[:9]
    gog_o, table_g, table_l, gain_o, proj_o, up_o, down_o = refs[9:16]
    rest = list(refs[16:])
    buf = {name: rest.pop(0) for name, _, _ in FIXED}
    eg = {name: rest.pop(0) for name, _ in TABLE}
    el = {name: rest.pop(0) for name, _ in TABLE}
    unit_bufs = []
    for _ in ALL_UNITS:
        unit_bufs.append([rest.pop(0) for _ in range(5)])
    load_sem, x_send, x_recv, ab_sem, g_sem, tg_sem, tl_sem, u_sem = rest
    ids, gain = buf["ids"], buf["gain"]
    og, dn, gig, pw, emb, up = (buf[n] for n in ("og", "dn", "gig", "pw", "emb", "up"))
    og2, slot, dh, norm, scale, r2 = (buf[n] for n in ("og2", "slot", "dh", "norm", "scale", "r2"))
    hot, ht, dat, da = (buf[n] for n in ("hot", "ht", "dat", "da"))
    dr, du, dut, dp, upart, pp = (buf[n] for n in ("dr", "du", "dut", "dp", "upart", "pp"))
    pr, gog, gp = (buf[n] for n in ("pr", "gog", "gp"))

    seq = lax.axis_index("seq")
    tp = lax.axis_index("tp")
    core = seq % 2
    other = 1 - core
    x = seq // 4
    y = (seq // 2) % 2 * 2 + tp % 2
    z = tp // 2
    spot = (x, y, z)

    def device(px, py, pz, pc):
        return ((px * 2 + py // 2) * 2 + pc, pz * 2 + py % 2)

    def device_at(axis, place):
        where = list(spot)
        where[axis] = place
        return device(*where, core)

    partner = device(x, y, z, other)

    barrier = pltpu.get_barrier_semaphore()
    pl.semaphore_signal(barrier, inc=1, device_id=partner, device_id_type=MESH)
    for ky, kz in PLANE:
        there = device(x, (y + ky) % 4, (z + kz) % 4, core)
        pl.semaphore_signal(barrier, inc=1, device_id=there, device_id_type=MESH)
    for k in FAR_FIRST:
        pl.semaphore_signal(barrier, inc=1, device_id=device_at(0, (x + k) % 4), device_id_type=MESH)
    loads = {}
    for n, group in enumerate(
        (
            (("og", og_h, og),),
            (("dn", dn_h, dn),),
            (("ids", ids_h, ids),),
            (("gig", gig_h, gig),),
            (("pw", pw_h, pw),),
            (("emb", emb_h, emb),),
            (("up", up_h, up),),
            (("own", go_h.at[tp], slot.at[tp]),),
            (("gain", gain_h, gain),),
        )
    ):
        for name, src, dst in group:
            loads[name] = pltpu.make_async_copy(src, dst, load_sem.at[n])
            loads[name].start()
    pl.semaphore_wait(barrier, 19)

    def to_group(src, dst, sem, offsets):
        for k in offsets:
            device = (seq, (tp + k) % 8)
            remote(src.at[(tp + k) % 8], dst.at[tp], ab_sem.at[sem], ab_sem.at[sem + 1], device).start()

    to_group(go_h, slot, 0, range(1, 8))

    def swap(n, src, dst):
        copy = remote(src, dst, x_send.at[n], x_recv.at[n], partner)
        copy.start()
        return copy

    loads["og"].wait()
    row, col = iota((256, 256), 0), iota((256, 256), 1)
    perm = (col == 8 * (row % 32) + row // 32).astype(BF)
    own, far = pl.ds(0, 256), pl.ds(256, 256)
    og2[own, :] = mm(perm, og[...]).astype(BF)
    x_og = swap(0, og2.at[own], og2.at[far])

    loads["dn"].wait()

    def dh_step(n, carry):
        at = pl.ds(pl.multiple_of(n * 256, 256), 256)
        dh[n] = mm_nt(og2[own, :], dn[at, :])
        return carry

    lax.fori_loop(0, 8, dh_step, 0)

    loads["ids"].wait()
    ids_v = ids[...]
    own_id = jnp.sum(jnp.where(iota((8, 256), 0) == tp, ids_v, 0), axis=0, keepdims=True)
    hot_own = (row == own_id).astype(BF)
    pick = (row == tp * 32 + col % 32).astype(BF)
    ids_here = mm(ids_v.astype(F32).astype(BF), pick)
    col8 = iota((8, 256), 1)
    prev = jnp.sum(jnp.where(iota((8, 256), 0) == col8 // 32 - 1, ids_here, 0.0), axis=0, keepdims=True)
    prev_id = jnp.where(iota((1, 256), 1) < 32, -1, prev.astype(jnp.int32))
    hot[...] = (row == prev_id).astype(BF)

    def table_of(bufs, gathered, sems):
        order = tuple(bufs[n] for n in ("src", "one", "recv1", "recv2"))
        return Table(order, gathered, spot, core, device, device_at, partner, sems)

    glob, loc = table_of(eg, table_g, tg_sem), table_of(el, table_l, tl_sem)

    def put_table(part, n, value):
        block = value.astype(BF).reshape(4, 2, 2, 16, 256)
        for c in range(2):
            for yh in range(2):
                for yl in range(2):
                    part[c, :, yh * 2 + yl, n] = block[:, yh, c, :, yl * 128 : yl * 128 + 128]

    def join(part, src):
        def step(i, carry):
            src[i] = (src[i].astype(F32) + part[core, i].astype(F32)).astype(BF)
            return carry

        lax.fori_loop(0, 4, step, 0)

    loads["gig"].wait()
    for n in range(4):
        put_table(eg["part"], n, mm(hot_own, gig[:, n * 256 : n * 256 + 256]))
    x_eg = swap(1, eg["part"].at[other], eg["src"])

    loads["pw"].wait()
    loads["emb"].wait()
    loads["own"].wait()
    loads["gain"].wait()
    x_eg.wait_recv()
    join(eg["part"], eg["src"])
    glob.start(0)
    seven = pl.ds(0, 7)
    await_recv(slot.at[seven], ab_sem.at[1], partner)

    square = jnp.zeros((256, 1), F32)
    slot_v = slot[...].reshape(256, 1024)
    for n in range(4):
        at = slice(n * 256, n * 256 + 256)
        u_part = mm(slot_v, pw[:, at]) + mm_tn(hot[...], emb[:, at])
        norm[:, at] = u_part
        square = square + jnp.sum(u_part * u_part, axis=1, keepdims=True)
    scale_v = lax.rsqrt(square * (1.0 / 1024.0) + 1e-05)
    scale[...] = jnp.broadcast_to(scale_v, (256, 128))
    for n in range(4):
        at = slice(n * 256, n * 256 + 256)
        normed = norm[:, at] * scale_v
        norm[:, at] = normed
        r2[own, at] = (normed * gain[:, at]).astype(BF)
    x_r = swap(2, r2.at[own], r2.at[far])

    loads["up"].wait()

    def h_swap(j):
        rows = pl.ds(pl.multiple_of(j * 256, 256), 256)
        return remote(
            ht.at[other, rows, own], ht.at[other, rows, far], x_send.at[6 + j], x_recv.at[6 + j], partner
        )

    def ff_step(j, carry):
        for k2 in range(2):
            k = j * 2 + k2
            at = pl.ds(pl.multiple_of(k * 256, 256), 256)
            rows = pl.ds(pl.multiple_of(k * 128, 128), 128)
            a = mm(r2[own, :], up[:, at])
            sig = jax.nn.sigmoid(a)
            h_t = (a * sig).astype(BF).T
            ht[0, rows, own] = h_t[:128]
            ht[1, rows, own] = h_t[128:]
            da_v = (dh[k] * sig * (1.0 + a * (1.0 - sig))).astype(BF)
            da[:, at] = da_v
            da_t = da_v.T
            dat[0, rows, own] = da_t[:128]
            dat[1, rows, own] = da_t[128:]
        h_swap(j).start()
        return carry

    lax.fori_loop(0, 4, ff_step, 0)
    glob.finish(0)
    glob.start(1)

    def units(src, table, first):
        return [
            Unit(src, t[:2], t[2], spot, device_at, unit_bufs[first + i], u_sem.at[first + i])
            for i, t in enumerate(table)
        ]

    d_units = units(dp, D_UNITS, 0)
    u_units = units(upart, U_UNITS, 3)
    p_units = units(pr, P_UNITS, 6)

    def big(lhs, rhs, out, n):
        at = slice(n * 256, n * 256 + 256)

        def step(g, carry):
            rows = pl.ds(pl.multiple_of(g * 512, 512), 512)
            v = mm(lhs[core, rows, :], rhs[:, at]).astype(BF).reshape(2, 2, 4, 2, 16, 256)
            for xx in range(2):
                for yh in range(2):
                    for yl in range(2):
                        out[2 * g + xx, yh * 2 + yl, :, :, at] = v[xx, yh, :, yl]
            return carry

        lax.fori_loop(0, 2, step, 0)

    for n in range(4):
        at = slice(n * 256, n * 256 + 256)
        dr[:, at] = mm_nt(da[...], up[at, :])
    x_og.wait_recv()
    for j in range(4):
        h_swap(j).wait_recv()
    x_da = swap(4, dat.at[other, :, own], dat.at[other, :, far])
    big(ht, og2, dp, 0)
    d_units[0].one.start()
    big(ht, og2, dp, 1)
    big(ht, og2, dp, 2)
    d_units[1].one.start()
    big(ht, og2, dp, 3)
    d_units[2].one.start()
    glob.finish(1)
    glob.start(2)
    x_r.wait_recv()
    x_da.wait_recv()
    big(dat, r2, upart, 0)
    u_units[0].one.start()
    big(dat, r2, upart, 1)
    big(dat, r2, upart, 2)
    u_units[1].one.start()
    big(dat, r2, upart, 3)
    u_units[2].one.start()
    gain_v = gain[...]

    def du_step(i, total):
        rows = pl.ds(pl.multiple_of(i * 32, 32), 32)
        dr_v = dr[rows, :]
        normed = norm[rows, :]
        product = dr_v * normed
        dn_v = dr_v * gain_v
        mean = jnp.sum(product * gain_v, axis=1, keepdims=True) * (1.0 / 1024.0)
        du_v = og2[rows, :].astype(F32) + scale[rows, 0:1] * (dn_v - normed * mean)
        du[rows, :] = du_v.astype(BF)
        return total + jnp.sum(product.reshape(4, 8, 1024), axis=0)

    gain_part = lax.fori_loop(0, 8, du_step, jnp.zeros((8, 1024), F32))
    for n in range(4):
        put_table(el["part"], n, mm(hot[...], du[:, n * 256 : n * 256 + 256]))
    x_el = swap(3, el["part"].at[other], el["src"])
    gp[0, core] = jnp.sum(gain_part, axis=0, keepdims=True)
    x_g = swap(5, gp.at[0, core], gp.at[0, core])
    for unit in d_units:
        unit.one.relay()
    for n in range(4):
        at = slice(n * 256, n * 256 + 256)
        dut[at, :] = du[:, at].T

    def gain_swap(step):
        axis = step - 1
        mine = gp.at[step, spot[axis]]
        for k in FAR_FIRST:
            device = device_at(axis, (spot[axis] + k) % 4)
            remote(mine, mine, g_sem.at[2 * axis], g_sem.at[2 * axis + 1], device).start()

    def gain_join(step):
        three = gp.at[step, pl.ds(0, 3)]
        await_recv(three, g_sem.at[2 * step - 1], partner)
        await_send(three, g_sem.at[2 * step - 2], partner)
        return gp[step, 0] + gp[step, 1] + gp[step, 2] + gp[step, 3]

    def p_swap(g):
        return remote(pp.at[other, g], pr.at[g], x_send.at[10 + g], x_recv.at[10 + g], partner)

    def proj_step(g, carry):
        rows = pl.ds(pl.multiple_of(g * 256, 256), 256)
        for n in range(2):
            lo, hi = slice(n * 256, n * 256 + 256), slice(512 + n * 256, 768 + n * 256)
            v_lo = mm(dut[rows, :], slot[:, :, lo].reshape(256, 256)).reshape(2, 2, 4, 2, 8, 256)
            v_hi = mm(dut[rows, :], slot[:, :, hi].reshape(256, 256)).reshape(2, 2, 4, 2, 8, 256)
            v = jnp.concatenate([v_lo, v_hi], axis=4).astype(BF)
            for c in range(2):
                for yh in range(2):
                    for yl in range(2):
                        pp[c, g, yh * 2 + yl, :, :, lo] = v[yh, c, :, yl]
        p_swap(g).start()
        return carry

    lax.fori_loop(0, 4, proj_step, 0)
    x_el.wait_recv()
    join(el["part"], el["src"])
    loc.start(0)
    x_g.wait_recv()
    x_g.wait_send()
    gp[1, x] = gp[0, 0] + gp[0, 1]
    gain_swap(1)
    for n in range(4):
        at = slice(n * 256, n * 256 + 256)
        gog[:, :, at] = mm_nt(du[...], pw[at, :]).astype(BF).reshape(8, 32, 256)
    own_back = pltpu.make_async_copy(gog.at[tp], gog_o.at[tp], load_sem.at[9])
    own_back.start()
    for g in range(4):
        p_swap(g).wait_recv()
    join(pp, pr)
    for unit in p_units:
        unit.one.start()
    for unit in u_units:
        unit.one.relay()
    glob.finish(2)
    glob.start(3)
    loc.finish(0)
    loc.start(1)
    for unit in p_units:
        unit.one.relay()
    for unit in d_units:
        unit.start2()
    gp[2, y] = gain_join(1)
    gain_swap(2)
    loc.finish(1)
    loc.start(2)
    for unit in u_units:
        unit.start2()
    for unit in p_units:
        unit.start2()
    for unit in d_units:
        unit.start3()
    loc.finish(2)
    loc.start(3)
    to_group(gog, gog_o, 2, (1, 2, 3))
    gp[3, z] = gain_join(2)
    gain_swap(3)
    for unit in u_units:
        unit.start3()
    for unit in p_units:
        unit.start3()
    to_group(gog, gog_o, 2, (4, 5, 6, 7))
    glob.finish(3)
    glob.start(4)
    for i, unit in enumerate(d_units):
        down_o[:, pl.ds(*D_UNITS[i][:2])] = unit.three.finish()
    gain_o[...] = gain_join(3)
    loc.finish(3)
    loc.start(4)
    for i, unit in enumerate(u_units):
        up_o[:, pl.ds(*U_UNITS[i][:2])] = unit.three.finish()
    for i, unit in enumerate(p_units):
        first, width, _ = P_UNITS[i]
        value = unit.three.finish()
        proj_o[:, pl.ds(first, width)] = value[:8]
        proj_o[:, pl.ds(512 + first, width)] = value[8:]
    glob.finish(4)
    glob.drain()
    for unit in d_units + u_units + p_units:
        unit.drain()
    await_send(slot.at[seven], ab_sem.at[0], partner)
    for copy in (x_og, x_eg, x_r, x_da, x_el):
        copy.wait_send()
    for i in range(4):
        h_swap(i).wait_send()
        p_swap(i).wait_send()
    await_recv(gog_o.at[seven], ab_sem.at[3], partner)
    own_back.wait()
    await_send(gog_o.at[seven], ab_sem.at[2], partner)
    loc.finish(4)
    loc.drain()


def finish(gog, table_g, table_l, gain, proj, up, down, gog_o, embg_o, embl_o, gain_o, proj_o, up_o, down_o, embg, embl, sem):
    pairs = ((gog, gog_o), (gain, gain_o), (proj, proj_o), (up, up_o), (down, down_o))
    copies = [pltpu.make_async_copy(src, dst, sem.at[n]) for n, (src, dst) in enumerate(pairs)]
    for copy in copies:
        copy.start()
    for n, (table, value, out) in enumerate(((table_g, embg, embg_o), (table_l, embl, embl_o))):
        for row in range(16):
            px, yh, c = row // 4, row // 2 % 2, row % 2
            for col in range(8):
                pz, yl = col // 2, col % 2
                value[row * 16 : row * 16 + 16, col * 128 : col * 128 + 128] = table[c, px, yh * 2 + yl, pz].astype(F32)
        copy = pltpu.make_async_copy(value, out, sem.at[5 + n])
        copy.start()
        copies.append(copy)
    for copy in copies:
        copy.wait()


def on_device(
    byte_ids,
    global_out,
    global_in_grad,
    out_grad,
    proj_weight,
    emb_local,
    norm_gain,
    up_weight,
    down_weight,
):
    scratch = [pltpu.VMEM(shape, kind) for _, shape, kind in FIXED]
    scratch += [pltpu.VMEM(shape, BF) for _, shape in TABLE] * 2
    for _, width, order in ALL_UNITS:
        scratch += unit_scratch(width, order)
    dma = pltpu.SemaphoreType.DMA
    scratch += [dma((n,)) for n in (N_LOADS, N_X, N_X, 4, 6, 10, 10)] + [dma((len(ALL_UNITS), 7))]
    vmem = pl.BlockSpec(memory_space=pltpu.VMEM)
    anywhere = pl.BlockSpec(memory_space=pl.ANY)
    parts = pl.pallas_call(
        kernel,
        out_shape=(
            pltpu.VMEM((8, 32, 1024), BF),
            pltpu.VMEM((2, 4, 4, 4, 16, 128), BF),
            pltpu.VMEM((2, 4, 4, 4, 16, 128), BF),
            pltpu.VMEM((1, 1024), F32),
            pltpu.VMEM((8, 1024), F32),
            pltpu.VMEM((16, 1024), F32),
            pltpu.VMEM((16, 1024), F32),
        ),
        in_specs=[pl.BlockSpec(memory_space=pltpu.HBM)] * 9,
        out_specs=[vmem] * 7,
        scratch_shapes=scratch,
        compiler_params=pltpu.CompilerParams(
            collective_id=0, has_side_effects=True, vmem_limit_bytes=52 * 1024 * 1024
        ),
    )(
        pltpu.with_memory_space_constraint(byte_ids.T, pltpu.HBM),
        global_out.reshape(8, 32, 1024),
        global_in_grad,
        out_grad,
        proj_weight,
        emb_local,
        pltpu.with_memory_space_constraint(norm_gain.reshape(1, 1024), pltpu.HBM),
        up_weight,
        down_weight,
    )
    out = jax.ShapeDtypeStruct
    gog, embg, embl, gain, proj, up, down = pl.pallas_call(
        finish,
        out_shape=(
            out((8, 32, 1024), BF),
            out((256, 1024), F32),
            out((256, 1024), F32),
            out((1, 1024), F32),
            out((8, 1024), F32),
            out((16, 1024), F32),
            out((16, 1024), F32),
        ),
        in_specs=[vmem] * 7,
        out_specs=[anywhere] * 7,
        scratch_shapes=[pltpu.VMEM((256, 1024), F32), pltpu.VMEM((256, 1024), F32), dma((7,))],
        compiler_params=pltpu.CompilerParams(vmem_limit_bytes=6 * 1024 * 1024),
    )(*parts)
    return gog.reshape(256, 1024), embg, embl, gain.reshape(1024), proj.T, up.T, down


def solution(mesh):
    placed = (
        P("seq", None),
        P("seq", "tp"),
        P("seq", "tp"),
        P(("seq", "tp"), None),
        P(),
        P(),
        P(),
        P(),
        P(),
    )
    return jax.shard_map(
        on_device,
        mesh=mesh,
        in_specs=placed,
        out_specs=(
            P("seq", "tp"),
            P(),
            P(),
            P(),
            P(None, ("seq", "tp")),
            P(None, ("seq", "tp")),
            P(("seq", "tp"), None),
        ),
        check_vma=False,
    )
```

time: 73.5 us -> 60 us (0.82)
  Pallas kernels: 70.9 us -> 59.2 us
  local copies, waits for them, and re-layouts: 1.38 us -> 0 us
    pallas_call x1, Pallas kernels: 69.3 us -> 57.6 us  [on_device(): pl.pallas_call(kernel, out_shape=(pltpu.VMEM((8, 32, 1024), BF), pltpu.VM...]
    unnamed x4 -> x0, local copies, waits for them, and re-layouts: 1.38 us -> none
where the time goes in v3:
time: 60 us; the launch traced here: 59.8 us
  Pallas kernels  59.2 us (99%)
  between operations  0.64 us (1%)
    pallas_call x1, Pallas kernels, on_device(): pl.pallas_call(kernel, out_shape=(pltpu.VMEM((8, 32, 1024), BF), pltpu.VM...  57.6 us
    pallas_call x1, Pallas kernels, on_device(): pl.pallas_call(finish, out_shape=(out((8, 32, 1024), BF), out((256, 1024)...  1.61 us

profile of v3, /device:TPU:1, one launch (start us, length us, event | category | flops | bytes accessed | tf_op | source)
XLA Modules:
  0.0 59.8 jit_solution(13382037922064476277)
XLA Ops:
  0.6 57.6 %shard_map.144 = (bf16[8,32,1024]{2,1,0:T(8,128)(2,1)S(1)}, bf16[2,4,4,4,16,128]{5,4,3,2,1,0:T(8,128)(2,1)S(1)}, bf16[2,4,4,4,16,128]{5,4,3,2,1,0:T(8,128)(2,1)S...) custom-call(s32[8,256]{1,0:T(8,128)} %bitcast.8, ...), custom_call_target="tpu_custom_call" | custom-call | tf_op jit(solution)/shard_map/pallas_call | solution.py:651
  58.2 1.6 %shard_map.145 = (bf16[8,32,1024]{2,1,0:T(8,128)(2,1)}, f32[256,1024]{1,0:T(8,128)}, f32[256,1024]{1,0:T(8,128)}, f32[1,1024]{1,0:T(1,128)}, f32[8,1024]{1,0:T(8...) custom-call(bf16[8,32,1024]{2,1,0:T(8,128)(2,1)S(1)} %get-tuple-element.21.gog, ...), custom_call_target="tpu_custom_call" | custom-call | tf_op jit(solution)/shard_map/pallas_call | solution.py:680

commit v4 on v3

--- a/solution.py
+++ b/solution.py
@@ -9,9 +9,9 @@
 F32 = jnp.float32
 MESH = pl.DeviceIdType.MESH
 ALL = slice(None)
-D_UNITS = ((0, 256, (0, 1, 2)), (256, 384, (1, 2, 0)), (640, 384, (2, 0, 1)))
+D_UNITS = ((0, 256, (1, 2, 0)), (256, 384, (2, 0, 1)), (640, 384, (0, 1, 2)))
 U_UNITS = ((0, 256, (0, 1, 2)), (256, 384, (1, 2, 0)), (640, 384, (2, 0, 1)))
-P_UNITS = ((0, 256, (0, 1, 2)), (256, 128, (1, 2, 0)), (384, 128, (2, 0, 1)))
+P_UNITS = ((0, 128, (0, 1, 2)), (128, 256, (1, 2, 0)), (384, 128, (2, 0, 1)))
 ALL_UNITS = D_UNITS + U_UNITS + P_UNITS
 FAR_FIRST = (2, 1, 3)
 PLANE = tuple((ky, kz) for ky in (2, 1, 3, 0) for kz in (2, 1, 3, 0) if ky or kz)
@@ -215,9 +215,10 @@
     ("pw", (1024, 1024), BF),
     ("emb", (256, 1024), BF),
     ("up", (1024, 2048), BF),
-    ("og2", (512, 1024), BF),
-    ("slot", (8, 32, 1024), BF),
-    ("dh", (8, 256, 256), F32),
+    ("ogp", (8, 2, 16, 1024), BF),
+    ("og2", (2, 8, 2, 16, 1024), BF),
+    ("slot", (256, 1024), BF),
+    ("slope", (8, 256, 256), F32),
     ("norm", (256, 1024), F32),
     ("scale", (256, 128), F32),
     ("r2", (512, 1024), BF),
@@ -232,7 +233,6 @@
     ("upart", (4, 4, 4, 16, 1024), BF),
     ("pp", (2, 4, 4, 4, 16, 512), BF),
     ("pr", (4, 4, 4, 16, 512), BF),
-    ("gog", (8, 32, 1024), BF),
     ("gp", (4, 4, 1, 1024), F32),
 )
 TABLE = (
@@ -242,7 +242,7 @@
     ("recv1", (3, 4, 4, 16, 128)),
     ("recv2", (15, 16, 128)),
 )
-N_LOADS, N_X = 10, 14
+N_LOADS, N_X = 10, 18
 
 
 def kernel(*refs):
@@ -258,10 +258,10 @@
     load_sem, x_send, x_recv, ab_sem, g_sem, tg_sem, tl_sem, u_sem = rest
     ids, gain = buf["ids"], buf["gain"]
     og, dn, gig, pw, emb, up = (buf[n] for n in ("og", "dn", "gig", "pw", "emb", "up"))
-    og2, slot, dh, norm, scale, r2 = (buf[n] for n in ("og2", "slot", "dh", "norm", "scale", "r2"))
+    og2, slot, slope, norm, scale, r2 = (buf[n] for n in ("og2", "slot", "slope", "norm", "scale", "r2"))
     hot, ht, dat, da = (buf[n] for n in ("hot", "ht", "dat", "da"))
     dr, du, dut, dp, upart, pp = (buf[n] for n in ("dr", "du", "dut", "dp", "upart", "pp"))
-    pr, gog, gp = (buf[n] for n in ("pr", "gog", "gp"))
+    pr, gp, ogp = (buf[n] for n in ("pr", "gp", "ogp"))
 
     seq = lax.axis_index("seq")
     tp = lax.axis_index("tp")
@@ -293,58 +293,46 @@
     for n, group in enumerate(
         (
             (("og", og_h, og),),
+            (("slot", go_h, slot),),
+            (("pw", pw_h, pw),),
+            (("ids", ids_h, ids),),
+            (("emb", emb_h, emb),),
+            (("gain", gain_h, gain),),
+            (("gig", gig_h, gig),),
+            (("up", up_h, up),),
             (("dn", dn_h, dn),),
-            (("ids", ids_h, ids),),
-            (("gig", gig_h, gig),),
-            (("pw", pw_h, pw),),
-            (("emb", emb_h, emb),),
-            (("up", up_h, up),),
-            (("own", go_h.at[tp], slot.at[tp]),),
-            (("gain", gain_h, gain),),
         )
     ):
         for name, src, dst in group:
             loads[name] = pltpu.make_async_copy(src, dst, load_sem.at[n])
             loads[name].start()
+
+    loads["og"].wait()
+    row, col = iota((256, 256), 0), iota((256, 256), 1)
+    own, far = pl.ds(0, 256), pl.ds(256, 256)
+    perm = (col == 8 * (row % 32) + row // 32).astype(BF)
+    ogp[...] = mm(perm, og[...]).astype(BF).reshape(8, 2, 16, 1024)
+    keep = pltpu.make_async_copy(ogp.at[tp], og2.at[0, tp], load_sem.at[9])
+    keep.start()
     pl.semaphore_wait(barrier, 19)
-
-    def to_group(src, dst, sem, offsets):
-        for k in offsets:
-            device = (seq, (tp + k) % 8)
-            remote(src.at[(tp + k) % 8], dst.at[tp], ab_sem.at[sem], ab_sem.at[sem + 1], device).start()
-
-    to_group(go_h, slot, 0, range(1, 8))
+    for half in range(2):
+        for k in range(1, 8):
+            there = (tp + k) % 8
+            remote(
+                ogp.at[there, half], og2.at[0, tp, half], ab_sem.at[0], ab_sem.at[1 + half], (seq, there)
+            ).start()
 
     def swap(n, src, dst):
         copy = remote(src, dst, x_send.at[n], x_recv.at[n], partner)
         copy.start()
         return copy
 
-    loads["og"].wait()
-    row, col = iota((256, 256), 0), iota((256, 256), 1)
-    perm = (col == 8 * (row % 32) + row // 32).astype(BF)
-    own, far = pl.ds(0, 256), pl.ds(256, 256)
-    og2[own, :] = mm(perm, og[...]).astype(BF)
-    x_og = swap(0, og2.at[own], og2.at[far])
-
-    loads["dn"].wait()
-
-    def dh_step(n, carry):
-        at = pl.ds(pl.multiple_of(n * 256, 256), 256)
-        dh[n] = mm_nt(og2[own, :], dn[at, :])
-        return carry
-
-    lax.fori_loop(0, 8, dh_step, 0)
-
     loads["ids"].wait()
     ids_v = ids[...]
-    own_id = jnp.sum(jnp.where(iota((8, 256), 0) == tp, ids_v, 0), axis=0, keepdims=True)
+    row8 = iota((8, 256), 0)
+    own_id = jnp.sum(jnp.where(row8 == tp, ids_v, 0), axis=0, keepdims=True)
     hot_own = (row == own_id).astype(BF)
-    pick = (row == tp * 32 + col % 32).astype(BF)
-    ids_here = mm(ids_v.astype(F32).astype(BF), pick)
-    col8 = iota((8, 256), 1)
-    prev = jnp.sum(jnp.where(iota((8, 256), 0) == col8 // 32 - 1, ids_here, 0.0), axis=0, keepdims=True)
-    prev_id = jnp.where(iota((1, 256), 1) < 32, -1, prev.astype(jnp.int32))
+    prev_id = jnp.sum(jnp.where(row8 == tp - 1, ids_v, 0), axis=0, keepdims=True) - (tp == 0).astype(jnp.int32)
     hot[...] = (row == prev_id).astype(BF)
 
     def table_of(bufs, gathered, sems):
@@ -374,19 +362,12 @@
 
     loads["pw"].wait()
     loads["emb"].wait()
-    loads["own"].wait()
+    loads["slot"].wait()
     loads["gain"].wait()
-    x_eg.wait_recv()
-    join(eg["part"], eg["src"])
-    glob.start(0)
-    seven = pl.ds(0, 7)
-    await_recv(slot.at[seven], ab_sem.at[1], partner)
-
     square = jnp.zeros((256, 1), F32)
-    slot_v = slot[...].reshape(256, 1024)
     for n in range(4):
         at = slice(n * 256, n * 256 + 256)
-        u_part = mm(slot_v, pw[:, at]) + mm_tn(hot[...], emb[:, at])
+        u_part = mm(slot[...], pw[:, at]) + mm_tn(hot[...], emb[:, at])
         norm[:, at] = u_part
         square = square + jnp.sum(u_part * u_part, axis=1, keepdims=True)
     scale_v = lax.rsqrt(square * (1.0 / 1024.0) + 1e-05)
@@ -397,14 +378,17 @@
         norm[:, at] = normed
         r2[own, at] = (normed * gain[:, at]).astype(BF)
     x_r = swap(2, r2.at[own], r2.at[far])
-
-    loads["up"].wait()
-
-    def h_swap(j):
+    x_eg.wait_recv()
+    join(eg["part"], eg["src"])
+    glob.start(0)
+
+    def t_swap(ref, base, j):
         rows = pl.ds(pl.multiple_of(j * 256, 256), 256)
         return remote(
-            ht.at[other, rows, own], ht.at[other, rows, far], x_send.at[6 + j], x_recv.at[6 + j], partner
+            ref.at[other, rows, own], ref.at[other, rows, far], x_send.at[base + j], x_recv.at[base + j], partner
         )
+
+    loads["up"].wait()
 
     def ff_step(j, carry):
         for k2 in range(2):
@@ -416,17 +400,33 @@
             h_t = (a * sig).astype(BF).T
             ht[0, rows, own] = h_t[:128]
             ht[1, rows, own] = h_t[128:]
-            da_v = (dh[k] * sig * (1.0 + a * (1.0 - sig))).astype(BF)
+            slope[k] = sig * (1.0 + a * (1.0 - sig))
+        t_swap(ht, 6, j).start()
+        return carry
+
+    lax.fori_loop(0, 4, ff_step, 0)
+
+    def da_step(j, carry):
+        for k2 in range(2):
+            k = j * 2 + k2
+            at = pl.ds(pl.multiple_of(k * 256, 256), 256)
+            rows = pl.ds(pl.multiple_of(k * 128, 128), 128)
+            da_v = (mm_nt(og2[0].reshape(256, 1024), dn[at, :]) * slope[k]).astype(BF)
             da[:, at] = da_v
             da_t = da_v.T
             dat[0, rows, own] = da_t[:128]
             dat[1, rows, own] = da_t[128:]
-        h_swap(j).start()
+        t_swap(dat, 10, j).start()
         return carry
 
-    lax.fori_loop(0, 4, ff_step, 0)
-    glob.finish(0)
-    glob.start(1)
+    loads["dn"].wait()
+    keep.wait()
+    seven = pl.ds(0, 7)
+    x_og = []
+    for half in range(2):
+        await_recv(og2.at[0, seven, half], ab_sem.at[1 + half], partner)
+        x_og.append(swap((0, 4)[half], og2.at[0, :, half], og2.at[1, :, half]))
+    lax.fori_loop(0, 2, da_step, 0)
 
     def units(src, table, first):
         return [
@@ -441,42 +441,41 @@
     def big(lhs, rhs, out, n):
         at = slice(n * 256, n * 256 + 256)
 
-        def step(g, carry):
-            rows = pl.ds(pl.multiple_of(g * 512, 512), 512)
-            v = mm(lhs[core, rows, :], rhs[:, at]).astype(BF).reshape(2, 2, 4, 2, 16, 256)
+        def step(g):
+            rows = pl.ds(g * 512, 512)
+            v = mm(lhs[core, rows, :], rhs(at)).astype(BF).reshape(2, 2, 4, 2, 16, 256)
             for xx in range(2):
                 for yh in range(2):
                     for yl in range(2):
                         out[2 * g + xx, yh * 2 + yl, :, :, at] = v[xx, yh, :, yl]
-            return carry
-
-        lax.fori_loop(0, 2, step, 0)
-
+
+        step(0)
+        step(1)
+
+    for j in range(4):
+        t_swap(ht, 6, j).wait_recv()
+    for copy in x_og:
+        copy.wait_recv()
+
+    def both_og(at):
+        return og2[:, :, :, :, at].reshape(512, 256)
+
+    def both_r(at):
+        return r2[:, at]
+
+    big(ht, both_og, dp, 0)
+    d_units[0].one.start()
+    big(ht, both_og, dp, 1)
+    big(ht, both_og, dp, 2)
+    d_units[1].one.start()
+    big(ht, both_og, dp, 3)
+    d_units[2].one.start()
+    glob.finish(0)
+    glob.start(1)
+    lax.fori_loop(2, 4, da_step, 0)
     for n in range(4):
         at = slice(n * 256, n * 256 + 256)
         dr[:, at] = mm_nt(da[...], up[at, :])
-    x_og.wait_recv()
-    for j in range(4):
-        h_swap(j).wait_recv()
-    x_da = swap(4, dat.at[other, :, own], dat.at[other, :, far])
-    big(ht, og2, dp, 0)
-    d_units[0].one.start()
-    big(ht, og2, dp, 1)
-    big(ht, og2, dp, 2)
-    d_units[1].one.start()
-    big(ht, og2, dp, 3)
-    d_units[2].one.start()
-    glob.finish(1)
-    glob.start(2)
-    x_r.wait_recv()
-    x_da.wait_recv()
-    big(dat, r2, upart, 0)
-    u_units[0].one.start()
-    big(dat, r2, upart, 1)
-    big(dat, r2, upart, 2)
-    u_units[1].one.start()
-    big(dat, r2, upart, 3)
-    u_units[2].one.start()
     gain_v = gain[...]
 
     def du_step(i, total):
@@ -486,7 +485,7 @@
         product = dr_v * normed
         dn_v = dr_v * gain_v
         mean = jnp.sum(product * gain_v, axis=1, keepdims=True) * (1.0 / 1024.0)
-        du_v = og2[rows, :].astype(F32) + scale[rows, 0:1] * (dn_v - normed * mean)
+        du_v = og2[0, i].reshape(32, 1024).astype(F32) + scale[rows, 0:1] * (dn_v - normed * mean)
         du[rows, :] = du_v.astype(BF)
         return total + jnp.sum(product.reshape(4, 8, 1024), axis=0)
 
@@ -498,6 +497,21 @@
     x_g = swap(5, gp.at[0, core], gp.at[0, core])
     for unit in d_units:
         unit.one.relay()
+    x_el.wait_recv()
+    join(el["part"], el["src"])
+    loc.start(0)
+    x_r.wait_recv()
+    for j in range(4):
+        t_swap(dat, 10, j).wait_recv()
+    big(dat, both_r, upart, 0)
+    u_units[0].one.start()
+    big(dat, both_r, upart, 1)
+    big(dat, both_r, upart, 2)
+    u_units[1].one.start()
+    big(dat, both_r, upart, 3)
+    u_units[2].one.start()
+    glob.finish(1)
+    glob.start(2)
     for n in range(4):
         at = slice(n * 256, n * 256 + 256)
         dut[at, :] = du[:, at].T
@@ -516,14 +530,14 @@
         return gp[step, 0] + gp[step, 1] + gp[step, 2] + gp[step, 3]
 
     def p_swap(g):
-        return remote(pp.at[other, g], pr.at[g], x_send.at[10 + g], x_recv.at[10 + g], partner)
+        return remote(pp.at[other, g], pr.at[g], x_send.at[14 + g], x_recv.at[14 + g], partner)
 
     def proj_step(g, carry):
         rows = pl.ds(pl.multiple_of(g * 256, 256), 256)
         for n in range(2):
             lo, hi = slice(n * 256, n * 256 + 256), slice(512 + n * 256, 768 + n * 256)
-            v_lo = mm(dut[rows, :], slot[:, :, lo].reshape(256, 256)).reshape(2, 2, 4, 2, 8, 256)
-            v_hi = mm(dut[rows, :], slot[:, :, hi].reshape(256, 256)).reshape(2, 2, 4, 2, 8, 256)
+            v_lo = mm(dut[rows, :], slot[:, lo]).reshape(2, 2, 4, 2, 8, 256)
+            v_hi = mm(dut[rows, :], slot[:, hi]).reshape(2, 2, 4, 2, 8, 256)
             v = jnp.concatenate([v_lo, v_hi], axis=4).astype(BF)
             for c in range(2):
                 for yh in range(2):
@@ -533,30 +547,23 @@
         return carry
 
     lax.fori_loop(0, 4, proj_step, 0)
-    x_el.wait_recv()
-    join(el["part"], el["src"])
-    loc.start(0)
     x_g.wait_recv()
     x_g.wait_send()
     gp[1, x] = gp[0, 0] + gp[0, 1]
     gain_swap(1)
     for n in range(4):
         at = slice(n * 256, n * 256 + 256)
-        gog[:, :, at] = mm_nt(du[...], pw[at, :]).astype(BF).reshape(8, 32, 256)
-    own_back = pltpu.make_async_copy(gog.at[tp], gog_o.at[tp], load_sem.at[9])
-    own_back.start()
+        gog_o[:, at] = mm_nt(du[...], pw[at, :]).astype(BF)
+    loc.finish(0)
+    loc.start(1)
     for g in range(4):
         p_swap(g).wait_recv()
     join(pp, pr)
     for unit in p_units:
         unit.one.start()
-    for unit in u_units:
-        unit.one.relay()
     glob.finish(2)
     glob.start(3)
-    loc.finish(0)
-    loc.start(1)
-    for unit in p_units:
+    for unit in u_units:
         unit.one.relay()
     for unit in d_units:
         unit.start2()
@@ -564,22 +571,22 @@
     gain_swap(2)
     loc.finish(1)
     loc.start(2)
+    for unit in p_units:
+        unit.one.relay()
     for unit in u_units:
-        unit.start2()
-    for unit in p_units:
         unit.start2()
     for unit in d_units:
         unit.start3()
     loc.finish(2)
     loc.start(3)
-    to_group(gog, gog_o, 2, (1, 2, 3))
     gp[3, z] = gain_join(2)
     gain_swap(3)
+    for unit in p_units:
+        unit.start2()
     for unit in u_units:
         unit.start3()
     for unit in p_units:
         unit.start3()
-    to_group(gog, gog_o, 2, (4, 5, 6, 7))
     glob.finish(3)
     glob.start(4)
     for i, unit in enumerate(d_units):
@@ -598,15 +605,14 @@
     glob.drain()
     for unit in d_units + u_units + p_units:
         unit.drain()
-    await_send(slot.at[seven], ab_sem.at[0], partner)
-    for copy in (x_og, x_eg, x_r, x_da, x_el):
+    for half in range(2):
+        await_send(ogp.at[seven, half], ab_sem.at[0], partner)
+    for copy in x_og + [x_eg, x_r, x_el]:
         copy.wait_send()
     for i in range(4):
-        h_swap(i).wait_send()
+        t_swap(ht, 6, i).wait_send()
+        t_swap(dat, 10, i).wait_send()
         p_swap(i).wait_send()
-    await_recv(gog_o.at[seven], ab_sem.at[3], partner)
-    own_back.wait()
-    await_send(gog_o.at[seven], ab_sem.at[2], partner)
     loc.finish(4)
     loc.drain()
 
@@ -645,13 +651,13 @@
     for _, width, order in ALL_UNITS:
         scratch += unit_scratch(width, order)
     dma = pltpu.SemaphoreType.DMA
-    scratch += [dma((n,)) for n in (N_LOADS, N_X, N_X, 4, 6, 10, 10)] + [dma((len(ALL_UNITS), 7))]
+    scratch += [dma((n,)) for n in (N_LOADS, N_X, N_X, 3, 6, 10, 10)] + [dma((len(ALL_UNITS), 7))]
     vmem = pl.BlockSpec(memory_space=pltpu.VMEM)
     anywhere = pl.BlockSpec(memory_space=pl.ANY)
     parts = pl.pallas_call(
         kernel,
         out_shape=(
-            pltpu.VMEM((8, 32, 1024), BF),
+            pltpu.VMEM((256, 1024), BF),
             pltpu.VMEM((2, 4, 4, 4, 16, 128), BF),
             pltpu.VMEM((2, 4, 4, 4, 16, 128), BF),
             pltpu.VMEM((1, 1024), F32),
@@ -667,7 +673,7 @@
         ),
     )(
         pltpu.with_memory_space_constraint(byte_ids.T, pltpu.HBM),
-        global_out.reshape(8, 32, 1024),
+        global_out,
         global_in_grad,
         out_grad,
         proj_weight,
@@ -680,7 +686,7 @@
     gog, embg, embl, gain, proj, up, down = pl.pallas_call(
         finish,
         out_shape=(
-            out((8, 32, 1024), BF),
+            out((256, 1024), BF),
             out((256, 1024), F32),
             out((256, 1024), F32),
             out((1, 1024), F32),
@@ -693,7 +699,7 @@
         scratch_shapes=[pltpu.VMEM((256, 1024), F32), pltpu.VMEM((256, 1024), F32), dma((7,))],
         compiler_params=pltpu.CompilerParams(vmem_limit_bytes=6 * 1024 * 1024),
     )(*parts)
-    return gog.reshape(256, 1024), embg, embl, gain.reshape(1024), proj.T, up.T, down
+    return gog, embg, embl, gain.reshape(1024), proj.T, up.T, down
 
 
 def solution(mesh):

time: 60 us -> 56.6 us (0.943); the launches traced: 59.8 us -> 55.6 us
  Pallas kernels: 59.2 us -> 54.9 us
    pallas_call x2, Pallas kernels: 59.2 us -> 54.9 us  [the longest x1 53.3 us: on_device(): pl.pallas_call(kernel, out_shape=(pltpu.VMEM((256, 1024), BF), pltpu.VMEM...]
where the time goes in v4:
time: 56.6 us; the launch traced here: 55.6 us
  Pallas kernels  54.9 us (97%)
  between operations  0.64 us (1%)
    pallas_call x1, Pallas kernels, on_device(): pl.pallas_call(kernel, out_shape=(pltpu.VMEM((256, 1024), BF), pltpu.VMEM...  53.3 us
    pallas_call x1, Pallas kernels, on_device(): pl.pallas_call(finish, out_shape=(out((256, 1024), BF), out((256, 1024),...  1.61 us

profile of v4, /device:TPU:1, one launch (start us, length us, event | category | flops | bytes accessed | tf_op | source)
XLA Modules:
  0.0 55.6 jit_solution(4123461943418001450)
XLA Ops:
  0.6 53.3 %shard_map.144 = (bf16[256,1024]{1,0:T(8,128)(2,1)S(1)}, bf16[2,4,4,4,16,128]{5,4,3,2,1,0:T(8,128)(2,1)S(1)}, bf16[2,4,4,4,16,128]{5,4,3,2,1,0:T(8,128)(2,1)S(1)...) custom-call(s32[8,256]{1,0:T(8,128)} %bitcast.5, ...), custom_call_target="tpu_custom_call" | custom-call | tf_op jit(solution)/shard_map/pallas_call | solution.py:657
  54.0 1.6 %shard_map.145 = (bf16[256,1024]{1,0:T(8,128)(2,1)}, f32[256,1024]{1,0:T(8,128)}, f32[256,1024]{1,0:T(8,128)}, f32[1,1024]{1,0:T(1,128)}, f32[8,1024]{1,0:T(8,12...) custom-call(bf16[256,1024]{1,0:T(8,128)(2,1)S(1)} %get-tuple-element.21.gog, ...), custom_call_target="tpu_custom_call" | custom-call | tf_op jit(solution)/shard_map/pallas_call | solution.py:686

commit v5 on v4

--- a/solution.py
+++ b/solution.py
@@ -11,7 +11,7 @@
 ALL = slice(None)
 D_UNITS = ((0, 256, (1, 2, 0)), (256, 384, (2, 0, 1)), (640, 384, (0, 1, 2)))
 U_UNITS = ((0, 256, (0, 1, 2)), (256, 384, (1, 2, 0)), (640, 384, (2, 0, 1)))
-P_UNITS = ((0, 128, (0, 1, 2)), (128, 256, (1, 2, 0)), (384, 128, (2, 0, 1)))
+P_UNITS = ((0, 128, (0, 1, 2)), (128, 256, (1, 2, 0)), (384, 128, (2, 1, 0)))
 ALL_UNITS = D_UNITS + U_UNITS + P_UNITS
 FAR_FIRST = (2, 1, 3)
 PLANE = tuple((ky, kz) for ky in (2, 1, 3, 0) for kz in (2, 1, 3, 0) if ky or kz)
@@ -62,14 +62,17 @@
         )
         return self.src.at[index + (ALL, pl.ds(*self.cols))]
 
+    def start_far(self):
+        remote(self.part(self.far, 0), self.buf.at[0], self.send, self.recv[0], self.to_right).start()
+        remote(self.part(self.far, 1), self.buf.at[1], self.send, self.recv[0], self.to_left).start()
+
+    def start_near(self):
+        remote(self.part(self.right, 1), self.buf.at[2], self.send, self.recv[1], self.to_right).start()
+        remote(self.part(self.left, 0), self.buf.at[3], self.send, self.recv[1], self.to_left).start()
+
     def start(self):
-        for src, n, sem, device in (
-            (self.part(self.far, 0), 0, 0, self.to_right),
-            (self.part(self.far, 1), 1, 0, self.to_left),
-            (self.part(self.right, 1), 2, 1, self.to_right),
-            (self.part(self.left, 0), 3, 1, self.to_left),
-        ):
-            remote(src, self.buf.at[n], self.send, self.recv[sem], device).start()
+        self.start_far()
+        self.start_near()
 
     def relay(self):
         await_recv(self.buf.at[pl.ds(0, 2)], self.recv[0], self.to_left)
@@ -560,31 +563,33 @@
         p_swap(g).wait_recv()
     join(pp, pr)
     for unit in p_units:
-        unit.one.start()
+        unit.one.start_far()
+    for unit in u_units:
+        unit.one.relay()
+    for unit in p_units:
+        unit.one.start_near()
+    for unit in d_units:
+        unit.start2()
+    for unit in p_units:
+        unit.one.relay()
+    loc.finish(1)
+    loc.start(2)
     glob.finish(2)
     glob.start(3)
     for unit in u_units:
-        unit.one.relay()
-    for unit in d_units:
         unit.start2()
     gp[2, y] = gain_join(1)
     gain_swap(2)
-    loc.finish(1)
-    loc.start(2)
     for unit in p_units:
-        unit.one.relay()
-    for unit in u_units:
         unit.start2()
+    loc.finish(2)
+    loc.start(3)
     for unit in d_units:
         unit.start3()
-    loc.finish(2)
-    loc.start(3)
+    for unit in u_units:
+        unit.start3()
     gp[3, z] = gain_join(2)
     gain_swap(3)
-    for unit in p_units:
-        unit.start2()
-    for unit in u_units:
-        unit.start3()
     for unit in p_units:
         unit.start3()
     glob.finish(3)

time: 56.6 us -> 55.9 us (0.988); the launches traced: 55.6 us -> 55.8 us
  no operation moved by 1% of the time
where the time goes in v5:
time: 55.9 us; the launch traced here: 55.8 us
  Pallas kernels  55.1 us (99%)
  between operations  0.64 us (1%)
    pallas_call x1, Pallas kernels, on_device(): pl.pallas_call(kernel, out_shape=(pltpu.VMEM((256, 1024), BF), pltpu.VMEM...  53.5 us
    pallas_call x1, Pallas kernels, on_device(): pl.pallas_call(finish, out_shape=(out((256, 1024), BF), out((256, 1024),...  1.61 us

profile of v5, /device:TPU:1, one launch (start us, length us, event | category | flops | bytes accessed | tf_op | source)
XLA Modules:
  0.0 55.8 jit_solution(16245099796479998932)
XLA Ops:
  0.6 53.5 %shard_map.144 = (bf16[256,1024]{1,0:T(8,128)(2,1)S(1)}, bf16[2,4,4,4,16,128]{5,4,3,2,1,0:T(8,128)(2,1)S(1)}, bf16[2,4,4,4,16,128]{5,4,3,2,1,0:T(8,128)(2,1)S(1)...) custom-call(s32[8,256]{1,0:T(8,128)} %bitcast.5, ...), custom_call_target="tpu_custom_call" | custom-call | tf_op jit(solution)/shard_map/pallas_call | solution.py:662
  54.2 1.6 %shard_map.145 = (bf16[256,1024]{1,0:T(8,128)(2,1)}, f32[256,1024]{1,0:T(8,128)}, f32[256,1024]{1,0:T(8,128)}, f32[1,1024]{1,0:T(1,128)}, f32[8,1024]{1,0:T(8,12...) custom-call(bf16[256,1024]{1,0:T(8,128)(2,1)S(1)} %get-tuple-element.21.gog, ...), custom_call_target="tpu_custom_call" | custom-call | tf_op jit(solution)/shard_map/pallas_call | solution.py:691

commit v6 on v5

--- a/solution.py
+++ b/solution.py
@@ -557,13 +557,13 @@
     for n in range(4):
         at = slice(n * 256, n * 256 + 256)
         gog_o[:, at] = mm_nt(du[...], pw[at, :]).astype(BF)
-    loc.finish(0)
-    loc.start(1)
     for g in range(4):
         p_swap(g).wait_recv()
     join(pp, pr)
     for unit in p_units:
         unit.one.start_far()
+    loc.finish(0)
+    loc.start(1)
     for unit in u_units:
         unit.one.relay()
     for unit in p_units:

time: 55.9 us -> 55.4 us (level)
  no operation moved by 1% of the time
where the time goes in v6:
time: 55.4 us; the launch traced here: 55.3 us
  Pallas kernels  54.6 us (99%)
  between operations  0.64 us (1%)
    pallas_call x1, Pallas kernels, on_device(): pl.pallas_call(kernel, out_shape=(pltpu.VMEM((256, 1024), BF), pltpu.VMEM...  53 us
    pallas_call x1, Pallas kernels, on_device(): pl.pallas_call(finish, out_shape=(out((256, 1024), BF), out((256, 1024),...  1.61 us

profile of v6, /device:TPU:1, one launch (start us, length us, event | category | flops | bytes accessed | tf_op | source)
XLA Modules:
  0.0 55.3 jit_solution(7581429347220456616)
XLA Ops:
  0.6 53.0 %shard_map.144 = (bf16[256,1024]{1,0:T(8,128)(2,1)S(1)}, bf16[2,4,4,4,16,128]{5,4,3,2,1,0:T(8,128)(2,1)S(1)}, bf16[2,4,4,4,16,128]{5,4,3,2,1,0:T(8,128)(2,1)S(1)...) custom-call(s32[8,256]{1,0:T(8,128)} %bitcast.5, ...), custom_call_target="tpu_custom_call" | custom-call | tf_op jit(solution)/shard_map/pallas_call | solution.py:662
  53.7 1.6 %shard_map.145 = (bf16[256,1024]{1,0:T(8,128)(2,1)}, f32[256,1024]{1,0:T(8,128)}, f32[256,1024]{1,0:T(8,128)}, f32[1,1024]{1,0:T(1,128)}, f32[8,1024]{1,0:T(8,12...) custom-call(bf16[256,1024]{1,0:T(8,128)(2,1)S(1)} %get-tuple-element.21.gog, ...), custom_call_target="tpu_custom_call" | custom-call | tf_op jit(solution)/shard_map/pallas_call | solution.py:691
